TPU v7x, 128 devices: a whole 4x4x4 slice. The times are simulated.
128 devices in a mesh: seq: 32 (over z, y, core), tp: 4 (over x).
Axes of the slice: x: 4, y: 4, z: 4, core: 2. Of those that a mesh axis runs over, the one named last changes fastest.
Arguments:
- states: bfloat16 [256, 3072], P(None, 'seq'), may hold values from -20 to 20
- norm_gain: bfloat16 [3072], P('seq'), may hold values from 0.25 to 1.75
- w_qkv: bfloat16 [3, 3072, 3072], P(None, 'seq', 'tp'), may hold values from -0.109375 to 0.109375
- w_out: bfloat16 [3072, 3072], P('tp', 'seq'), may hold values from -0.109375 to 0.109375
- cache: bfloat16 [768, 2, 64, 3072], P('seq', None, None, 'tp'), may hold values from -400 to 400
- context_len: int32 [256], replicated, may hold values from 1 to 4096, as said below
- block_owner: int32 [768], P('seq'), may hold values from 0 to 256, as said below
- block_index: int32 [768], P('seq'), may hold values from 0 to 63, as said below
Outputs:
- hidden: bfloat16 [256, 3072], P('tp', 'seq')
- updated: bfloat16 [768, 2, 64, 3072], P('seq', None, None, 'tp')
Inputs may be any that keep to these rules, and one draw needn't show every extreme that they name: `context_len`: A request of length n owns exactly ceil(n / 64) pool blocks, with block_index 0, 1, ... once each; at least one pool block is unused. `context_len`: exactly 4 requests own 64/2 blocks or more; every other request owns at most 2 blocks, all on one index of seq. `block_owner`: the value 256 marks an unused block. `block_index`: 0 for an unused block.
All inputs are finite; a program needn't handle non-finite values.
Results may differ from a plain program's by a relative error of at most 0.0068.
Values may be sent and summed in bfloat16 or wider, within the bound.
A program may use at most 128 MiB of HBM per device.

v0:
```python
import jax
import jax.numpy as jnp
from jax import lax
from jax.sharding import PartitionSpec as P

HEAD_DIM = 96


EPSILON = 1e-05
NEG_FLOOR = -1e30


def combined_all(part, axis, combine):
    gathered = jax.tree.map(lambda a: lax.all_gather(a, axis), part)

    def take(source):
        return jax.tree.map(lambda a: lax.dynamic_index_in_dim(a, source, 0, False), gathered)

    return lax.fori_loop(
        1, lax.axis_size(axis), lambda source, state: combine(state, take(source)), take(0)
    )


def rotate(values, positions):
    half_dim = HEAD_DIM // 2
    frequency = 10000.0 ** (-jnp.arange(half_dim, dtype=jnp.float32) * 2.0 / HEAD_DIM)
    angles = positions.astype(jnp.float32)[:, None] * frequency[None, :]
    cosine = jnp.cos(angles)[:, None, :]
    sine_part = jnp.sin(angles)[:, None, :]
    front_half = values[..., :half_dim]
    back_half = values[..., half_dim:]
    return jnp.concatenate(
        [front_half * cosine - back_half * sine_part, back_half * cosine + front_half * sine_part],
        axis=-1,
    )


def finish(projected, positions):
    row_count = projected.shape[0]
    columns = projected.shape[2]
    head_count = columns // HEAD_DIM
    query = rotate(
        projected[:, 0].reshape(row_count, head_count, HEAD_DIM), positions
    ) * HEAD_DIM ** (-0.5)
    keys_new = rotate(projected[:, 1].reshape(row_count, head_count, HEAD_DIM), positions)
    return (
        query.astype(jnp.bfloat16).reshape(row_count, columns),
        keys_new.astype(jnp.bfloat16).reshape(row_count, columns),
        projected[:, 2].astype(jnp.bfloat16),
    )


def join(earlier, later):
    highest = jnp.maximum(earlier[0], later[0])
    left_scale = jnp.exp(earlier[0] - highest)
    right_scale = jnp.exp(later[0] - highest)
    return (
        highest,
        earlier[1] * left_scale + later[1] * right_scale,
        earlier[2] * jnp.repeat(left_scale, HEAD_DIM, axis=1)
        + later[2] * jnp.repeat(right_scale, HEAD_DIM, axis=1),
    )


def shards(states, norm_gain, w_qkv, w_out, cache, context_len, block_owner, block_index):
    requests = states.shape[0]
    seq_count = lax.axis_size("seq")
    wide_states = states.astype(jnp.float32)
    sum_squares = lax.psum(jnp.sum(wide_states * wide_states, axis=1), "seq")
    inverse = lax.rsqrt(sum_squares / (states.shape[1] * seq_count) + EPSILON)
    normed = (wide_states * inverse[:, None] * norm_gain.astype(jnp.float32)[None, :]).astype(
        jnp.bfloat16
    )
    positions = context_len - 1
    local_term = jnp.einsum("rd,cdh->rch", normed, w_qkv, preferred_element_type=jnp.float32)
    projected = lax.psum(local_term, "seq")
    query, keys_new, values_new = finish(projected, positions)
    blocks, _, tokens, columns = cache.shape
    head_count = columns // HEAD_DIM
    block_live = block_owner < requests
    owner_row = jnp.minimum(block_owner, requests - 1)
    last_position = positions[owner_row]
    block_hit = block_live & (block_index == last_position // tokens)
    slot_hit = block_hit[:, None] & (
        jnp.arange(tokens, dtype=jnp.int32)[None, :] == (last_position % tokens)[:, None]
    )
    fresh_rows = jnp.stack([keys_new[owner_row], values_new[owner_row]], axis=1)
    updated = jnp.where(slot_hit[:, None, :, None], fresh_rows[:, :, None, :], cache)
    query_rows = query[owner_row].reshape(blocks, head_count, HEAD_DIM)
    key_cache = updated[:, 0].reshape(blocks, tokens, head_count, HEAD_DIM)
    value_cache = updated[:, 1].reshape(blocks, tokens, head_count, HEAD_DIM)
    scores = jnp.einsum("bhd,bthd->bht", query_rows, key_cache, preferred_element_type=jnp.float32)
    token_position = block_index[:, None] * tokens + jnp.arange(tokens, dtype=jnp.int32)[None, :]
    visible = block_live[:, None] & (token_position < context_len[owner_row][:, None])
    masked = jnp.where(visible[:, None, :], scores, NEG_FLOOR)
    block_max = jnp.max(masked, axis=-1)
    weights = jnp.where(visible[:, None, :], jnp.exp(masked - block_max[..., None]), 0.0).astype(
        jnp.bfloat16
    )
    block_sum = jnp.sum(weights.astype(jnp.float32), axis=-1)
    block_out = jnp.einsum(
        "bht,bthd->bhd", weights, value_cache, preferred_element_type=jnp.float32
    ).reshape(blocks, columns)
    segment = jnp.where(block_live, block_owner, requests)
    member = segment[None, :] == jnp.arange(requests, dtype=jnp.int32)[:, None]
    local_max = jnp.max(jnp.where(member[:, :, None], block_max[None, :, :], NEG_FLOOR), axis=1)
    factor = jnp.exp(block_max - local_max[owner_row])
    member_matrix = member.astype(jnp.float32)
    totals = jnp.dot(member_matrix, block_sum * factor, precision=lax.Precision.HIGHEST)
    outputs = jnp.dot(
        member_matrix,
        block_out * jnp.repeat(factor, HEAD_DIM, axis=1),
        precision=lax.Precision.HIGHEST,
    )
    merged = combined_all((local_max, totals, outputs), "seq", join)
    attended = (merged[2] / jnp.repeat(merged[1], HEAD_DIM, axis=1)).astype(jnp.bfloat16)
    terms = jnp.dot(attended, w_out, preferred_element_type=jnp.float32)
    summed = lax.psum_scatter(terms, "tp", scatter_dimension=0, tiled=True)
    row_count = summed.shape[0]
    residual_rows = lax.dynamic_slice_in_dim(
        wide_states, lax.axis_index("tp") * row_count, row_count, 0
    )
    hidden = (summed + residual_rows).astype(jnp.bfloat16)
    return (hidden, updated)


def solution(mesh):
    return jax.shard_map(
        shards,
        mesh=mesh,
        in_specs=(
            P(None, "seq"),
            P("seq"),
            P(None, "seq", "tp"),
            P("tp", "seq"),
            P("seq", None, None, "tp"),
            P(),
            P("seq"),
            P("seq"),
        ),
        out_specs=(P("tp", "seq"), P("seq", None, None, "tp")),
        check_vma=False,
    )
```

profile of v0, /device:TPU:1, one launch (start us, length us, event | category | flops | bytes accessed | tf_op | source)
XLA Modules:
  0.0 398.0 jit_solution(8305740966183515385)
XLA Ops:
  8.1 65.1 %psum.14 = f32[256]{0:T(256)S(1)} all-reduce(f32[256]{0:T(256)S(1)} %multiply_reduce_fusion), channel_id=1, replica_groups=mesh['seq'=32,'tp'=4] {'seq'}, use_global_device_ids=true, to_apply=%region_1.0 | all-reduce | flops 256 | bytes 2048 | tf_op jit(solution)/shard_map/psum | solution.py:69
  73.9 2.8 fusion.12
  78.7 106.4 %all-reduce.2.cloned.1.call-done = f32[256,3,768]{2,0,1:T(8,128)} async-done(((f32[256,3,768]{2,0,1:T(8,128)}), f32[256,3,768]{2,0,1:T(8,128)}) %all-reduce.2.cloned.1.call-update) | async-done | bytes 2359312 | tf_op jit(solution)/shard_map/psum | solution.py:76
  185.1 1.5 fusion.28
  190.9 2.7 broadcast_select_fusion
  193.6 2.2 fusion.27
  196.5 6.4 %reshape_squeeze.14 = bf16[24,64,8,96]{3,2,1,0:T(8,128)(2,1)} reshape(bf16[24,1,64,768]{3,2,1,0:T(8,128)(2,1)} %get-tuple-element.239) | data formatting | bytes 4718592 | tf_op jit(solution)/shard_map/reshape;squeeze | solution.py:90
  205.0 1.7 gather_fusion.1
  206.8 3.6 fusion.5
  210.8 4.3 %reshape_squeeze.15 = bf16[24,64,8,96]{3,2,1,0:T(8,128)(2,1)} reshape(bf16[24,1,64,768]{3,2,1,0:T(8,128)(2,1)S(1)} %get-tuple-element.238) | data formatting | bytes 4718592 | tf_op jit(solution)/shard_map/reshape;squeeze | solution.py:91
  215.9 2.8 fusion.3
  218.9 1.5 fusion.17
  220.7 25.8 %all-gather.1 = f32[8192,8]{0,1:T(8,128)S(1)} all-gather(f32[256,8]{0,1:T(8,128)S(1)} %fusion.18), channel_id=3, replica_groups=mesh['seq'=32,'tp'=4] {'seq'}, dimensions={0}, use_global_device_ids=true | all-gather | bytes 270336 | tf_op jit(solution)/shard_map/all_gather | solution.py:14
  246.5 22.3 %all-gather = f32[8192,8]{0,1:T(8,128)S(1)} all-gather(f32[256,8]{0,1:T(8,128)S(1)} %select_reduce_fusion), channel_id=2, replica_groups=mesh['seq'=32,'tp'=4] {'seq'}, dimensions={0}, use_global_device_ids=true | all-gather | bytes 270336 | tf_op jit(solution)/shard_map/all_gather | solution.py:14
  268.8 44.9 %all-gather.5.cloned.1.call-done = f32[8192,768]{1,0:T(8,128)} async-done(((f32[256,768]{1,0:T(8,128)}), f32[8192,768]{1,0:T(8,128)}) %all-gather.5.cloned.1.call-update) | async-done | bytes 25165840 | tf_op jit(solution)/shard_map/all_gather | solution.py:14
  315.1 56.6 %while.19 = (s32[]{:T(128)}, f32[256,8]{0,1:T(8,128)S(1)}, f32[256,8]{0,1:T(8,128)S(1)}, f32[256,768]{0,1:T(8,128)S(1)}, f32[32,256,8]{1,2,0:T(8,128)S(1)}, /*in...) while((s32[]{:T(128)}, f32[256,8]{0,1:T(8,128)S(1)}, ...), condition=%wide.region_7.8_spmd, body=%wide.region_6.7_spmd.sunk | while | flops 602117 | bytes 5587095 | solution.py:19
  315.2 1.2 constant_dynamic-slice_fusion.2
  317.0 1.2 constant_dynamic-slice_fusion.2
  318.8 1.2 constant_dynamic-slice_fusion.2
  320.7 1.2 constant_dynamic-slice_fusion.2
  322.5 1.2 constant_dynamic-slice_fusion.2
  324.3 1.2 constant_dynamic-slice_fusion.2
  326.1 1.2 constant_dynamic-slice_fusion.2
  327.9 1.2 constant_dynamic-slice_fusion.2
  329.8 1.2 constant_dynamic-slice_fusion.2
  331.6 1.2 constant_dynamic-slice_fusion.2
  333.4 1.2 constant_dynamic-slice_fusion.2
  335.2 1.2 constant_dynamic-slice_fusion.2
  337.1 1.2 constant_dynamic-slice_fusion.2
  338.9 1.2 constant_dynamic-slice_fusion.2
  340.7 1.2 constant_dynamic-slice_fusion.2
  342.5 1.2 constant_dynamic-slice_fusion.2
  344.4 1.2 constant_dynamic-slice_fusion.2
  346.2 1.2 constant_dynamic-slice_fusion.2
  348.0 1.2 constant_dynamic-slice_fusion.2
  349.8 1.2 constant_dynamic-slice_fusion.2
  351.7 1.2 constant_dynamic-slice_fusion.2
  353.5 1.2 constant_dynamic-slice_fusion.2
  355.3 1.2 constant_dynamic-slice_fusion.2
  357.1 1.2 constant_dynamic-slice_fusion.2
  359.0 1.2 constant_dynamic-slice_fusion.2
  360.8 1.2 constant_dynamic-slice_fusion.2
  362.6 1.2 constant_dynamic-slice_fusion.2
  364.4 1.2 constant_dynamic-slice_fusion.2
  366.3 1.2 constant_dynamic-slice_fusion.2
  368.1 1.2 constant_dynamic-slice_fusion.2
  369.9 1.2 constant_dynamic-slice_fusion.2
  372.8 17.1 %reduce-scatter.4.cloned.1.call-done = f32[64,96]{1,0:T(8,128)} async-done(((f32[256,96]{1,0:T(8,128)}), f32[64,96]{1,0:T(8,128)}) %reduce-scatter.4.cloned.1.call-update) | async-done | bytes 24592
  (160 shorter events, 34.9 us)
Async XLA Ops:
  7.2 66.7 %copy-start = (bf16[3,96,768]{2,1,0:T(8,128)(2,1)S(1)}, bf16[3,96,768]{2,1,0:T(8,128)(2,1)}, u32[]{:S(2)}) copy-start(bf16[3,96,768]{2,1,0:T(8,128)(2,1)} %param.12) | copy-start | bytes 1327108
  7.2 69.5 %copy-start.1 = (s32[256]{0:T(256)S(1)}, s32[256]{0:T(256)}, u32[]{:S(2)}) copy-start(s32[256]{0:T(256)} %param.15) | copy-start | bytes 3076
  7.2 69.5 %copy-start.5 = (s32[24]{0:T(128)S(1)}, s32[24]{0:T(128)}, u32[]{:S(2)}) copy-start(s32[24]{0:T(128)} %param.16) | copy-start | bytes 292
  7.2 177.9 %all-reduce.2.cloned.1.call-start = ((), (), s32[]{:S(2)}) async-start(), calls=%async_computation.1 | async-start | bytes 4718592 | tf_op jit(solution)/shard_map/psum | solution.py:76
  8.1 70.1 %copy-start.6 = (s32[24]{0:T(128)S(1)}, s32[24]{0:T(128)}, u32[]{:S(2)}) copy-start(s32[24]{0:T(128)} %param.17) | copy-start | bytes 292
  76.7 237.0 %all-gather.5.cloned.1.call-start = ((), (), s32[]{:S(2)}) async-start(), calls=%async_computation.2 | async-start | bytes 25952256 | tf_op jit(solution)/shard_map/all_gather | solution.py:14
  193.6 2.9 copy-start.2
  220.5 169.4 %reduce-scatter.4.cloned.1.call-start = ((), (), s32[]{:S(2)}) async-start(), calls=%async_computation.3 | async-start | bytes 163840
  315.1 56.7 %copy-start.4 = (bf16[768,96]{0,1:T(8,128)(2,1)S(1)}, bf16[768,96]{0,1:T(8,128)(2,1)}, u32[]{:S(2)}) copy-start(bf16[768,96]{0,1:T(8,128)(2,1)} %param.13) | copy-start | bytes 442372
  315.1 57.7 %copy-start.3 = (bf16[256,96]{0,1:T(8,128)(2,1)S(1)}, bf16[256,96]{0,1:T(8,128)(2,1)}, u32[]{:S(2)}) copy-start(bf16[256,96]{0,1:T(8,128)(2,1)} %param.10) | copy-start | bytes 147460
Sparse Core Ops, SparseCore 0:
  76.8 108.2 all-reduce.1
  220.6 92.9 all-gather.4
  372.9 16.9 reduce-scatter.3
where the time goes:
time: 402 us; the launch traced here: 398 us
  waiting for transfers between devices  168 us (42%)
  blocking collectives  113 us (28%)
  local copies, waits for them, and re-layouts  71.3 us (18%)
  other arithmetic  18 us (4%)
  between operations  14.1 us (4%)
  matrix products  11.8 us (3%)
    psum x1, waiting for transfers between devices, shards(): projected = lax.psum(local_term, 'seq')  106 us
    psum x1, blocking collectives, shards(): sum_squares = lax.psum(jnp.sum(wide_states * wide_states, axis=1), 'seq')  65.1 us
    all_gather x2, blocking collectives, combined_all(): gathered = jax.tree.map(lambda a: lax.all_gather(a, axis), part)  48.1 us
    dynamic_slice x65, local copies, waits for them, and re-layouts, take(): lax.dynamic_index_in_dim(a, source, 0, False)  46.3 us
    all_gather x1, waiting for transfers between devices, combined_all(): gathered = jax.tree.map(lambda a: lax.all_gather(a, axis), part)  44.9 us
    unnamed x4, waiting for transfers between devices  17.1 us
    add x31, other arithmetic, join(): earlier[2] * jnp.repeat(left_scale, HEAD_DIM, axis=1)  9.66 us
  transfers between devices with their start and end apart: 3, of which 3 were waited for; matrix products, arithmetic and copies ran while one was open for 1% of the time, Pallas kernels for 0%

commit v1 on v0

v1 whole, which is shorter than its diff:
```python
import functools

import jax
import jax.numpy as jnp
import numpy as np
from jax import lax
from jax.experimental import pallas as pl
from jax.experimental.pallas import tpu as pltpu
from jax.sharding import PartitionSpec as P

HEAD_DIM = 96
EPSILON = 1e-05
NEG_FLOOR = -1e30
GROUP = 8
LANES = 128
SIDE = 4
LONG_LIMIT = 31 * 64
LONG_REQS = 4
SLOTS = 24


def place():
    me = lax.axis_index("seq")
    core = me % 2
    y = (me // 2) % SIDE
    z = me // (2 * SIDE)
    first = z * (1 - core) + y * core
    second = y * (1 - core) + z * core

    def device(a, b):
        zz = a * (1 - core) + b * core
        yy = b * (1 - core) + a * core
        return (zz * SIDE + yy) * 2 + core

    primary = [device((first + i) % SIDE, second) for i in range(1, SIDE)]
    secondary = [device(first, (second + i) % SIDE) for i in range(1, SIDE)]
    partner = me + 1 - 2 * core
    return core, first, second, partner, primary, secondary


def send(src, dst, send_sem, recv_sem, axis, to):
    copy = pltpu.make_async_remote_copy(
        src_ref=src,
        dst_ref=dst,
        send_sem=send_sem,
        recv_sem=recv_sem,
        device_id={axis: to},
        device_id_type=pl.DeviceIdType.MESH,
    )
    copy.start()
    return copy


def greet(axis, others):
    barrier = pltpu.get_barrier_semaphore()
    for other in others:
        pl.semaphore_signal(
            barrier, inc=1, device_id={axis: other}, device_id_type=pl.DeviceIdType.MESH
        )


def halves(total):
    high = total.astype(jnp.bfloat16).astype(jnp.float32)
    lane = lax.broadcasted_iota(jnp.int32, total.shape, total.ndim - 1)
    return jnp.where(lane < LANES // 2, high, total - high).astype(jnp.bfloat16)


def whole(pair):
    pair = pair.astype(jnp.float32)
    return pair + pltpu.roll(pair, LANES // 2, pair.ndim - 1)


def rotated(values, cosine, sine, is_front):
    width = values.shape[-1]
    half = HEAD_DIM // 2
    other = jnp.where(
        is_front, pltpu.roll(values, width - half, 1), pltpu.roll(values, half, 1)
    )
    return values * cosine + other * sine


def project_kernel(
    context_ref, owner_ref, states_ref, gain_ref, w_ref, frequency_ref, out_ref,
    own, snd0, rcv0, snd1, rcv1, snd2, rcv2, gathered,
    sem0, sem1s, sem1r, sem2s, sem2r, sem3s, sem3r, sem4s, sem4r, sem5,
):
    core, first, second, partner, primary, secondary = place()
    greet("seq", [partner] + primary + secondary)

    parts, _, columns = w_ref.shape
    width = parts * columns
    rows = snd0.shape[0] * GROUP

    def local(half):
        rows_ref = states_ref[pl.ds(pl.multiple_of(half * rows, rows), rows), :]
        wide = rows_ref.astype(jnp.float32)
        total = jnp.sum(wide * wide, axis=1, keepdims=True)
        scaled = (wide * gain_ref[...].astype(jnp.float32)).astype(jnp.bfloat16)
        return scaled, jnp.broadcast_to(total, (rows, LANES))

    scaled, total = local(1 - core)
    for part in range(parts):
        term = jnp.dot(scaled, w_ref[part], preferred_element_type=jnp.float32)
        snd0[:, :, part * columns : (part + 1) * columns] = term.reshape(
            rows // GROUP, GROUP, columns
        ).astype(jnp.bfloat16)
    snd0[:, :, width:] = halves(total).reshape(rows // GROUP, GROUP, LANES)
    pl.semaphore_wait(pltpu.get_barrier_semaphore(), 7)
    copy0 = send(snd0, rcv0, sem0.at[0], sem0.at[1], "seq", partner)

    scaled, total = local(core)
    for part in range(parts):
        term = jnp.dot(scaled, w_ref[part], preferred_element_type=jnp.float32)
        own[:, :, part * columns : (part + 1) * columns] = term.reshape(
            rows // GROUP, GROUP, columns
        )
    own[:, :, width:] = total.reshape(rows // GROUP, GROUP, LANES)
    copy0.wait()

    copies = []
    for i in range(1, SIDE):
        there = ((first + i) % SIDE) * SIDE
        chunk = pl.ds(there, SIDE)
        snd1[i - 1, :, :, :width] = (
            own[chunk, :, :width] + rcv0[chunk, :, :width].astype(jnp.float32)
        ).astype(jnp.bfloat16)
        snd1[i - 1, :, :, width:] = halves(own[chunk, :, width:] + whole(rcv0[chunk, :, width:]))
        copies.append(
            send(
                snd1.at[i - 1], rcv1.at[i - 1], sem1s.at[i - 1], sem1r.at[i - 1],
                "seq", primary[i - 1],
            )
        )
    here = (core * SIDE + first) * SIDE + second
    row = lax.broadcasted_iota(jnp.int32, (GROUP, columns), 0)
    position = jnp.zeros((GROUP, columns), jnp.int32)
    for i in range(GROUP):
        position = jnp.where(row == i, context_ref[here * GROUP + i] - 1, position)
    angle = position.astype(jnp.float32) * frequency_ref[...]
    cosine = jnp.cos(angle)
    is_front = lax.broadcasted_iota(jnp.int32, (GROUP, columns), 1) % HEAD_DIM < HEAD_DIM // 2
    sine = jnp.where(is_front, -jnp.sin(angle), jnp.sin(angle))
    slot = lax.broadcasted_iota(jnp.int32, (SLOTS, 32 * GROUP), 0)
    wanted = jnp.zeros((SLOTS, 32 * GROUP), jnp.int32)
    for i in range(SLOTS):
        wanted = jnp.where(slot == i, owner_ref[i], wanted)
    pick = jnp.where(
        lax.broadcasted_iota(jnp.int32, (SLOTS, 32 * GROUP), 1) == wanted, 1.0, 0.0
    ).astype(jnp.bfloat16)

    mine = pl.ds(first * SIDE, SIDE)
    total = own[mine, :, width:] + whole(rcv0[mine, :, width:])
    own[mine, :, :width] = own[mine, :, :width] + rcv0[mine, :, :width].astype(jnp.float32)
    for copy in copies:
        copy.wait()
    for i in range(1, SIDE):
        total = total + whole(rcv1[i - 1, :, :, width:])
    own[mine, :, width:] = total

    base = first * SIDE
    copies = []
    for i in range(1, SIDE):
        there = (second + i) % SIDE
        term = own[base + there, :, :width]
        for k in range(SIDE - 1):
            term = term + rcv1[k, there, :, :width].astype(jnp.float32)
        snd2[i - 1, :, :width] = term.astype(jnp.bfloat16)
        snd2[i - 1, :, width:] = halves(own[base + there, :, width:])
        copies.append(
            send(
                snd2.at[i - 1], rcv2.at[i - 1], sem2s.at[i - 1], sem2r.at[i - 1],
                "seq", secondary[i - 1],
            )
        )
    term = own[base + second, :, :width]
    for k in range(SIDE - 1):
        term = term + rcv1[k, second, :, :width].astype(jnp.float32)
    total = own[base + second, :, width:]
    for copy in copies:
        copy.wait()
    for k in range(SIDE - 1):
        term = term + rcv2[k, :, :width].astype(jnp.float32)
        total = total + whole(rcv2[k, :, width:])
    inverse = lax.rsqrt(total / (HEAD_DIM * 32) + EPSILON)[:, :1]
    query = rotated(term[:, :columns] * inverse, cosine, sine, is_front) * HEAD_DIM ** (-0.5)
    key = rotated(term[:, columns : 2 * columns] * inverse, cosine, sine, is_front)
    value = term[:, 2 * columns :] * inverse
    gathered[core, first, second, :, :columns] = query.astype(jnp.bfloat16)
    gathered[core, first, second, :, columns : 2 * columns] = key.astype(jnp.bfloat16)
    gathered[core, first, second, :, 2 * columns :] = value.astype(jnp.bfloat16)

    block = gathered.at[core, first, second]
    copies = [
        send(block, block, sem3s.at[i], sem3r.at[i], "seq", secondary[i]) for i in range(SIDE - 1)
    ]
    for copy in copies:
        copy.wait()
    block = gathered.at[core, first]
    copies = [
        send(block, block, sem4s.at[i], sem4r.at[i], "seq", primary[i]) for i in range(SIDE - 1)
    ]
    for copy in copies:
        copy.wait()
    block = gathered.at[core]
    copy = send(block, block, sem5.at[0], sem5.at[1], "seq", partner)
    copy.wait()
    for part in range(parts):
        piece = gathered[:, :, :, :, part * columns : (part + 1) * columns]
        piece = piece.astype(jnp.float32).reshape(32 * GROUP, columns).astype(jnp.bfloat16)
        out_ref[:, part * columns : (part + 1) * columns] = jnp.dot(
            pick, piece, preferred_element_type=jnp.float32
        ).astype(jnp.bfloat16)


def attend_kernel(
    context_ref, owner_ref, index_ref, rows_ref, cache_ref, updated_ref, out_ref, stats_ref,
    buffer, scores, sem_in, sem_out,
):
    blocks, _, tokens, columns = cache_ref.shape
    heads = columns // HEAD_DIM
    requests = context_ref.shape[0]
    loads = []
    for j in range(blocks):
        load = pltpu.make_async_copy(cache_ref.at[j], buffer.at[j], sem_in.at[j])
        load.start()
        loads.append(load)
    head_mask = (
        lax.broadcasted_iota(jnp.int32, (heads, columns), 1) // HEAD_DIM
        == lax.broadcasted_iota(jnp.int32, (heads, columns), 0)
    )
    group = 16
    row = lax.broadcasted_iota(jnp.int32, (group, columns), 0)
    lane = lax.broadcasted_iota(jnp.int32, (heads, LANES), 1)
    owners = []
    seen = []
    owner_lanes = jnp.full((heads, LANES), requests, jnp.int32)
    stores = []
    for j in range(blocks):
        owner = owner_ref[j]
        live = owner < requests
        last = context_ref[jnp.minimum(owner, requests - 1)] - 1
        start = index_ref[j] * tokens
        visible = jnp.where(live, last + 1 - start, 0)
        hit = live & (index_ref[j] == last // tokens)
        place_in = last % tokens
        owners.append(owner)
        seen.append(visible)
        owner_lanes = jnp.where(lane == j, owner, owner_lanes)
        base = pl.multiple_of((place_in // group) * group, group)
        target = jnp.where(hit, place_in - base, -1)
        loads[j].wait()
        for c in range(2):
            fresh = rows_ref[j : j + 1, (c + 1) * columns : (c + 2) * columns]
            old = buffer[j, c, pl.ds(base, group), :]
            buffer[j, c, pl.ds(base, group), :] = jnp.where(
                row == target, fresh.astype(jnp.float32), old.astype(jnp.float32)
            ).astype(jnp.bfloat16)
        store = pltpu.make_async_copy(buffer.at[j], updated_ref.at[j], sem_out.at[j])
        store.start()
        stores.append(store)
        query = rows_ref[j : j + 1, :columns].astype(jnp.float32)
        spread = jnp.where(head_mask, query, 0.0).astype(jnp.bfloat16)
        scores[j] = lax.dot_general(
            spread, buffer[j, 0], (((1,), (1,)), ((), ())), preferred_element_type=jnp.float32
        )
    token = lax.broadcasted_iota(jnp.int32, (heads, tokens), 1)
    masked = []
    peaks = jnp.full((heads, LANES), NEG_FLOOR, jnp.float32)
    for j in range(blocks):
        value = jnp.where(token < seen[j], scores[j], NEG_FLOOR)
        masked.append(value)
        peak = jnp.max(value, axis=1, keepdims=True)
        peaks = jnp.where(lane == j, peak, peaks)
    group_peaks = jnp.zeros((heads, LANES), jnp.float32)
    sums = jnp.zeros((heads, LANES), jnp.float32)
    weights = []
    for j in range(blocks):
        same = owner_lanes == owners[j]
        peak = jnp.max(jnp.where(same, peaks, NEG_FLOOR), axis=1, keepdims=True)
        weight = jnp.where(token < seen[j], jnp.exp(masked[j] - peak), 0.0).astype(jnp.bfloat16)
        weights.append(weight)
        group_peaks = jnp.where(lane == j, peak, group_peaks)
        sums = jnp.where(
            lane == j, jnp.sum(weight.astype(jnp.float32), axis=1, keepdims=True), sums
        )
    group_sums = jnp.zeros((heads, LANES), jnp.float32)
    leads = jnp.zeros((heads, LANES), jnp.float32)
    for j in range(blocks):
        same = owner_lanes == owners[j]
        total = jnp.sum(jnp.where(same, sums, 0.0), axis=1, keepdims=True)
        group_sums = jnp.where(lane == j, total, group_sums)
        earlier = jnp.max(jnp.where(same & (lane < j), 1.0, 0.0), axis=1, keepdims=True)
        leads = jnp.where(lane == j, 1.0 - earlier, leads)
        inverse = jnp.where(total > 0.0, 1.0 / jnp.where(total > 0.0, total, 1.0), 0.0)
        piece = jnp.dot(weights[j], buffer[j, 1], preferred_element_type=jnp.float32)
        piece = jnp.where(head_mask, piece * inverse, 0.0)
        out_ref[j : j + 1, :] = jnp.sum(piece, axis=0, keepdims=True).astype(jnp.bfloat16)
    quarter = LANES // 4
    stats = jnp.where(
        lane < quarter,
        group_peaks,
        jnp.where(
            lane < 2 * quarter,
            pltpu.roll(group_sums, quarter, 1),
            jnp.where(
                lane < 3 * quarter,
                pltpu.roll(leads, 2 * quarter, 1),
                pltpu.roll(owner_lanes.astype(jnp.float32), 3 * quarter, 1),
            ),
        ),
    )
    stats_ref[...] = stats
    for store in stores:
        store.wait()


def combine_kernel(
    context_ref, rows_ref, stats_ref, w_ref, states_ref, out_ref,
    pool, table, terms, arrived,
    sem1s, sem1r, sem2s, sem2r, sem3, sem4s, sem4r,
):
    core, first, second, partner, primary, secondary = place()
    tp = lax.axis_index("tp")
    sides = [(tp + i) % SIDE for i in range(1, SIDE)]
    greet("seq", [partner] + primary + secondary)
    greet("tp", sides)
    slots, columns = rows_ref.shape
    heads = columns // HEAD_DIM
    requests = context_ref.shape[0] * context_ref.shape[1]
    padded = pool.shape[3]
    quarter = LANES // 4
    own_rows = pool.at[core, first, second, pl.ds(0, slots)]
    own_rows[...] = rows_ref[...]
    table[core, first, second] = stats_ref[...]
    pool[:, :, :, slots:, :] = jnp.zeros(
        (2, SIDE, SIDE, padded - slots, columns), jnp.bfloat16
    )
    context = context_ref[...]
    ids = lax.broadcasted_iota(jnp.int32, context.shape, 0) * context.shape[1] + (
        lax.broadcasted_iota(jnp.int32, context.shape, 1)
    )
    candidates = jnp.where(context > LONG_LIMIT, ids, -1).astype(jnp.float32)
    long_ids = []
    for _ in range(LONG_REQS):
        top = jnp.max(jnp.max(candidates, axis=1, keepdims=True), axis=0, keepdims=True)
        long_ids.append(top)
        candidates = jnp.where(candidates == top, -1.0, candidates)
    pl.semaphore_wait(pltpu.get_barrier_semaphore(), 10)

    copies = []
    for i in range(SIDE - 1):
        source = pool.at[core, first, second, pl.ds(0, slots)]
        copies.append(send(source, source, sem1s.at[0, i], sem1r.at[0, i], "seq", secondary[i]))
        source = table.at[core, first, second]
        copies.append(send(source, source, sem1s.at[1, i], sem1r.at[1, i], "seq", secondary[i]))
    for copy in copies:
        copy.wait()
    copies = []
    for i in range(SIDE - 1):
        source = pool.at[core, first, :, pl.ds(0, slots)]
        copies.append(send(source, source, sem2s.at[0, i], sem2r.at[0, i], "seq", primary[i]))
        source = table.at[core, first]
        copies.append(send(source, source, sem2s.at[1, i], sem2r.at[1, i], "seq", primary[i]))
    for copy in copies:
        copy.wait()
    source = pool.at[core, :, :, pl.ds(0, slots)]
    copies = [send(source, source, sem3.at[0], sem3.at[1], "seq", partner)]
    source = table.at[core]
    copies.append(send(source, source, sem3.at[2], sem3.at[3], "seq", partner))
    for copy in copies:
        copy.wait()

    lane = lax.broadcasted_iota(jnp.int32, (heads, LANES), 1)
    fields = [[] for _ in range(4)]
    devices = 2 * SIDE * SIDE
    for start in range(0, devices, 4):
        tiles = []
        for k in range(4):
            d = start + k
            tiles.append(table[d // (SIDE * SIDE), (d // SIDE) % SIDE, d % SIDE])
        for f in range(4):
            merged = jnp.zeros((heads, LANES), jnp.float32)
            for k in range(4):
                shift = ((k - f) * quarter) % LANES
                tile = tiles[k] if shift == 0 else pltpu.roll(tiles[k], shift, 1)
                merged = jnp.where(lane // quarter == k, tile, merged)
            fields[f].append(merged)
    peaks, sums, leads, owners = [jnp.concatenate(f, axis=1) for f in fields]
    used = lax.broadcasted_iota(jnp.int32, owners.shape, 1) % quarter < slots
    owners = jnp.where(used, owners, float(requests))

    high_rows = []
    low_rows = []
    is_long = jnp.zeros(owners.shape, jnp.bool_)
    for l in range(LONG_REQS):
        match = owners == long_ids[l]
        is_long = is_long | match
        peak = jnp.max(jnp.where(match, peaks, NEG_FLOOR), axis=1, keepdims=True)
        mass = jnp.where(match, sums * jnp.exp(jnp.where(match, peaks, NEG_FLOOR) - peak), 0.0)
        weight = mass / jnp.sum(jnp.where(match, mass * leads, 0.0), axis=1, keepdims=True)
        high = weight.astype(jnp.bfloat16)
        high_rows.append(high.astype(jnp.float32))
        low_rows.append(weight - high.astype(jnp.float32))
    request = lax.broadcasted_iota(jnp.int32, (requests, owners.shape[1]), 0).astype(jnp.float32)
    short_owner = jnp.where(is_long, float(requests), owners)[:1]
    member = jnp.where(request == short_owner, 1.0, 0.0).astype(jnp.bfloat16)
    extra = jnp.concatenate(high_rows + low_rows, axis=0).astype(jnp.bfloat16)
    values = (
        pool[...].astype(jnp.float32).reshape(devices * padded, columns).astype(jnp.bfloat16)
    )
    attended = jnp.dot(member, values, preferred_element_type=jnp.float32)
    weighted = jnp.dot(extra, values, preferred_element_type=jnp.float32)
    head_mask = (
        lax.broadcasted_iota(jnp.int32, (heads, columns), 1) // HEAD_DIM
        == lax.broadcasted_iota(jnp.int32, (heads, columns), 0)
    )
    row = lax.broadcasted_iota(jnp.int32, (requests, 1), 0).astype(jnp.float32)
    half = LONG_REQS * heads
    for l in range(LONG_REQS):
        both = weighted[l * heads : (l + 1) * heads] + weighted[
            half + l * heads : half + (l + 1) * heads
        ]
        line = jnp.sum(jnp.where(head_mask, both, 0.0), axis=0, keepdims=True)
        attended = jnp.where(row == long_ids[l], line, attended)
    product = jnp.dot(
        attended.astype(jnp.bfloat16), w_ref[...], preferred_element_type=jnp.float32
    )
    share = requests // SIDE
    terms[...] = product.reshape(SIDE, share, product.shape[1])
    copies = [
        send(
            terms.at[sides[i]], arrived.at[i], sem4s.at[i], sem4r.at[i], "tp", sides[i]
        )
        for i in range(SIDE - 1)
    ]
    total = terms[tp] + states_ref[
        pl.ds(pl.multiple_of(tp * share, share), share), :
    ].astype(jnp.float32)
    for copy in copies:
        copy.wait()
    for i in range(SIDE - 1):
        total = total + arrived[i]
    out_ref[...] = total.astype(jnp.bfloat16)


def shards(states, norm_gain, w_qkv, w_out, cache, context_len, block_owner, block_index):
    requests = states.shape[0]
    parts, depth, columns = w_qkv.shape
    width = parts * columns
    wide = width + LANES
    blocks = cache.shape[0]
    heads = columns // HEAD_DIM
    half_dim = HEAD_DIM // 2
    base = 10000.0 ** (-np.arange(half_dim, dtype=np.float64) * 2.0 / HEAD_DIM)
    frequency = jnp.asarray(np.tile(base, 2 * heads).astype(np.float32)[None, :])
    vmem = pl.BlockSpec(memory_space=pltpu.VMEM)
    smem = pl.BlockSpec(memory_space=pltpu.SMEM)
    hbm = pl.BlockSpec(memory_space=pl.ANY)
    dma = pltpu.SemaphoreType.DMA
    bf16 = jnp.bfloat16
    n = SIDE - 1
    rows = pl.pallas_call(
        project_kernel,
        name="project",
        out_shape=jax.ShapeDtypeStruct((blocks, width), bf16),
        in_specs=[smem, smem, vmem, vmem, vmem, vmem],
        out_specs=vmem,
        scratch_shapes=[
            pltpu.VMEM((16, GROUP, wide), jnp.float32),
            pltpu.VMEM((16, GROUP, wide), bf16),
            pltpu.VMEM((16, GROUP, wide), bf16),
            pltpu.VMEM((n, SIDE, GROUP, wide), bf16),
            pltpu.VMEM((n, SIDE, GROUP, wide), bf16),
            pltpu.VMEM((n, GROUP, wide), bf16),
            pltpu.VMEM((n, GROUP, wide), bf16),
            pltpu.VMEM((2, SIDE, SIDE, GROUP, width), bf16),
            dma((2,)),
            dma((n,)), dma((n,)), dma((n,)), dma((n,)),
            dma((n,)), dma((n,)), dma((n,)), dma((n,)),
            dma((2,)),
        ],
        compiler_params=pltpu.CompilerParams(collective_id=0, has_side_effects=True),
    )(context_len, block_owner, states, norm_gain[None, :], w_qkv, frequency)

    updated, slot_rows, stats = pl.pallas_call(
        attend_kernel,
        name="attend",
        out_shape=(
            jax.ShapeDtypeStruct(cache.shape, bf16),
            jax.ShapeDtypeStruct((blocks, columns), bf16),
            jax.ShapeDtypeStruct((heads, LANES), jnp.float32),
        ),
        in_specs=[smem, smem, smem, vmem, hbm],
        out_specs=(hbm, vmem, vmem),
        scratch_shapes=[
            pltpu.VMEM(cache.shape, bf16),
            pltpu.VMEM((blocks, heads, cache.shape[2]), jnp.float32),
            dma((blocks,)),
            dma((blocks,)),
        ],
    )(context_len, block_owner, block_index, rows, cache)

    hidden = pl.pallas_call(
        combine_kernel,
        name="combine",
        out_shape=jax.ShapeDtypeStruct((requests // SIDE, states.shape[1]), bf16),
        in_specs=[vmem] * 5,
        out_specs=vmem,
        scratch_shapes=[
            pltpu.VMEM((2, SIDE, SIDE, LANES // 4, columns), bf16),
            pltpu.VMEM((2, SIDE, SIDE, heads, LANES), jnp.float32),
            pltpu.VMEM((SIDE, requests // SIDE, states.shape[1]), jnp.float32),
            pltpu.VMEM((n, requests // SIDE, states.shape[1]), jnp.float32),
            dma((2, n)), dma((2, n)), dma((2, n)), dma((2, n)),
            dma((4,)),
            dma((n,)), dma((n,)),
        ],
        compiler_params=pltpu.CompilerParams(collective_id=1, has_side_effects=True),
    )(context_len.reshape(2, requests // 2), slot_rows, stats, w_out, states)
    return (hidden, updated)


def solution(mesh):
    return jax.shard_map(
        shards,
        mesh=mesh,
        in_specs=(
            P(None, "seq"),
            P("seq"),
            P(None, "seq", "tp"),
            P("tp", "seq"),
            P("seq", None, None, "tp"),
            P(),
            P("seq"),
            P("seq"),
        ),
        out_specs=(P("tp", "seq"), P("seq", None, None, "tp")),
        check_vma=False,
    )
```

time: 402 us -> 69.7 us (0.17)
  waiting for transfers between devices: 168 us -> 0 us
  blocking collectives: 113 us -> 0 us
  local copies, waits for them, and re-layouts: 71.3 us -> 3.69 us
  Pallas kernels: 0 us -> 65.1 us
  other arithmetic: 18 us -> 0 us
  between operations: 14.1 us -> 0.67 us
  matrix products: 11.8 us -> 0 us
    psum x1 -> x0, waiting for transfers between devices: 106 us -> none  [shards(): projected = lax.psum(local_term, 'seq')]
    pallas_call x0 -> x3, Pallas kernels: none -> 65.1 us  [the longest x1 34.1 us: shards(): pl.pallas_call(project_kernel, name='project', out_shape=jax.ShapeDtypeSt...]
    psum x1 -> x0, blocking collectives: 65.1 us -> none  [shards(): sum_squares = lax.psum(jnp.sum(wide_states * wide_states, axis=1), 'seq')]
    all_gather x2 -> x0, blocking collectives: 48.1 us -> none  [combined_all(): gathered = jax.tree.map(lambda a: lax.all_gather(a, axis), part)]
    dynamic_slice x65 -> x0, local copies, waits for them, and re-layouts: 46.3 us -> none  [take(): lax.dynamic_index_in_dim(a, source, 0, False)]
    all_gather x1 -> x0, waiting for transfers between devices: 44.9 us -> none  [combined_all(): gathered = jax.tree.map(lambda a: lax.all_gather(a, axis), part)]
    unnamed x4 -> x0, waiting for transfers between devices: 17.1 us -> none
    dot_general x5 -> x0, matrix products: 10.9 us -> none  [the longest x1 3.6 us: shards(): jnp.einsum('bhd,bthd->bht', query_rows, key_cache, preferred_element_type...]
  transfers between devices with their start and end apart: 3 -> 0, of which waited for: 3 -> 0; matrix products, arithmetic and copies ran while one was open for 1% -> 0% of each run, Pallas kernels for 0% -> 0%
where the time goes in v1:
time: 69.7 us; the launch traced here: 69.4 us
  Pallas kernels  65.1 us (93%)
  local copies, waits for them, and re-layouts  3.69 us (5%)
    pallas_call x1, Pallas kernels, shards(): pl.pallas_call(project_kernel, name='project', out_shape=jax.ShapeDtypeSt...  34.1 us
    pallas_call x1, Pallas kernels, shards(): pl.pallas_call(combine_kernel, name='combine', out_shape=jax.ShapeDtypeSt...  23 us
    pallas_call x1, Pallas kernels, shards(): pl.pallas_call(attend_kernel, name='attend', out_shape=(jax.ShapeDtypeStr...  7.98 us
    unnamed x5, local copies, waits for them, and re-layouts  3.69 us

profile of v1, /device:TPU:1, one launch (start us, length us, event | category | flops | bytes accessed | tf_op | source)
XLA Modules:
  0.0 69.4 jit_solution(17853999645916693639)
XLA Ops:
  0.6 0.0 copy-start
  0.6 1.6 %copy.11.states_ref = bf16[256,96]{1,0:T(8,128)(2,1)} copy(bf16[256,96]{0,1:T(8,128)(2,1)} %param.9) | data formatting | bytes 98304 | tf_op args[0]
  2.2 34.1 %project.1.rows_ref = bf16[24,2304]{1,0:T(8,128)(2,1)} custom-call(s32[256]{0:T(256)} %context_ref.3, s32[24]{0:T(128)} %owner_ref.3, bf16[256,96]{1,0:T(8,128)(2,1)} %copy.11.states_ref, bf16[1,96]{1,0:T(2,128)(2,1)} %bitcast.3, bf16[3,96,768]{2,1,0:T(8,128)(2,1)} %w_ref.2, f32[1,768]{1,0:T(1,128)} %constant.2.clone.frequency_ref), custom_call_target="tpu_custom_call" | custom-call | tf_op jit(solution)/shard_map/project/pallas_call | solution.py:462
  36.3 8.0 %attend.1 = (bf16[24,2,64,768]{3,2,1,0:T(8,128)(2,1)}, bf16[24,768]{1,0:T(8,128)(2,1)}, f32[8,128]{1,0:T(8,128)}) custom-call(s32[256]{0:T(256)} %context_ref.3, s32[24]{0:T(128)} %owner_ref.3, s32[24]{0:T(128)} %index_ref.1, bf16[24,2304]{1,0:T(8,128)(2,1)} %project.1.rows_ref, bf16[24,2,64,768]{3,2,1,0:T(8,128)(2,1)} %cache_ref.1), custom_call_target="tpu_custom_call" | custom-call | tf_op jit(solution)/shard_map/attend/pallas_call | solution.py:485
  44.3 0.0 copy-done
  44.3 0.8 %copy.12.w_ref = bf16[768,96]{1,0:T(8,128)(2,1)} copy(bf16[768,96]{0,1:T(8,128)(2,1)S(1)} %copy-done) | data formatting | bytes 294912 | tf_op args[3]
  45.1 23.0 %combine.1 = bf16[64,96]{1,0:T(8,128)(2,1)} custom-call(s32[2,128]{1,0:T(2,128)} %bitcast.2, bf16[24,768]{1,0:T(8,128)(2,1)} %get-tuple-element.5.rows_ref, f32[8,128]{1,0:T(8,128)} %get-tuple-element.6.stats_ref, bf16[768,96]{1,0:T(8,128)(2,1)} %copy.12.w_ref, bf16[256,96]{1,0:T(8,128)(2,1)} %copy.11.states_ref), custom_call_target="tpu_custom_call" | custom-call | tf_op jit(solution)/shard_map/combine/pallas_call | solution.py:503
  68.1 1.3 %copy.15 = bf16[64,96]{1,0:T(8,128)(2,1)} copy(bf16[64,96]{1,0:T(8,128)(2,1)} %combine.1) | data formatting | bytes 24576
Async XLA Ops:
  0.6 43.7 %copy-start = (bf16[768,96]{0,1:T(8,128)(2,1)S(1)}, bf16[768,96]{0,1:T(8,128)(2,1)}, u32[]{:S(2)}) copy-start(bf16[768,96]{0,1:T(8,128)(2,1)} %param.12) | copy-start | bytes 442372

commit v2 on v0

v2 whole, which is shorter than its diff:
```python
import functools

import jax
import jax.numpy as jnp
import numpy as np
from jax import lax
from jax.experimental import pallas as pl
from jax.experimental.pallas import tpu as pltpu
from jax.sharding import PartitionSpec as P

HEAD_DIM = 96
EPSILON = 1e-05
NEG_FLOOR = -1e30
GROUP = 8
LANES = 128
SIDE = 4
LONG_LIMIT = 31 * 64
LONG_REQS = 4
ORDER = (2, 1, 3)
ARRIVAL = (0, 2, 1)
ROW_GROUP = 16


def place():
    me = lax.axis_index("seq")
    core = me % 2
    y = (me // 2) % SIDE
    z = me // (2 * SIDE)
    first = z * (1 - core) + y * core
    second = y * (1 - core) + z * core

    def device(a, b):
        zz = a * (1 - core) + b * core
        yy = b * (1 - core) + a * core
        return (zz * SIDE + yy) * 2 + core

    primary = [device((first + i) % SIDE, second) for i in range(1, SIDE)]
    secondary = [device(first, (second + i) % SIDE) for i in range(1, SIDE)]
    partner = me + 1 - 2 * core
    return core, first, second, partner, primary, secondary


def send(src, dst, send_sem, recv_sem, axis, to):
    copy = pltpu.make_async_remote_copy(
        src_ref=src,
        dst_ref=dst,
        send_sem=send_sem,
        recv_sem=recv_sem,
        device_id={axis: to},
        device_id_type=pl.DeviceIdType.MESH,
    )
    copy.start()
    return copy


def greet(axis, others):
    barrier = pltpu.get_barrier_semaphore()
    for other in others:
        pl.semaphore_signal(
            barrier, inc=1, device_id={axis: other}, device_id_type=pl.DeviceIdType.MESH
        )


def halves(total):
    high = total.astype(jnp.bfloat16).astype(jnp.float32)
    lane = lax.broadcasted_iota(jnp.int32, total.shape, total.ndim - 1)
    return jnp.where(lane < LANES // 2, high, total - high).astype(jnp.bfloat16)


def whole(pair):
    pair = pair.astype(jnp.float32)
    return pair + pltpu.roll(pair, LANES // 2, pair.ndim - 1)


def rotated(values, cosine, sine, is_front):
    width = values.shape[-1]
    half = HEAD_DIM // 2
    other = jnp.where(
        is_front, pltpu.roll(values, width - half, 1), pltpu.roll(values, half, 1)
    )
    return values * cosine + other * sine


class Gather:
    def __init__(self, ref, sems, where, part=None):
        self.ref, self.part = ref, part
        self.core, self.first, self.second, self.partner, self.primary, self.secondary = where
        self.near_s, self.near_r, self.far_s, self.far_r, self.swap_s, self.swap_r = sems
        self.far = {}
        self.swaps = []

    def view(self, *index):
        if self.part is None:
            return self.ref.at[index]
        fill = (slice(None),) * (3 - len(index))
        return self.ref.at[index + fill + (pl.ds(0, self.part),)]

    def forward(self, i, block):
        for k in range(SIDE - 1):
            self.far[i, k] = send(
                block, block, self.far_s.at[i, k], self.far_r.at[i, k], "seq", self.primary[k]
            )

    def start(self):
        block = self.view(self.core, self.first, self.second)
        self.near = [
            send(block, block, self.near_s.at[i], self.near_r.at[i], "seq", self.secondary[i])
            for i in range(SIDE - 1)
        ]
        self.forward(0, block)

    def relay(self):
        for i in ARRIVAL:
            self.near[i].wait_recv()
            self.forward(
                i + 1,
                self.view(self.core, self.first, (self.second + SIDE - 1 - i) % SIDE),
            )
        self.swap(0, self.view(self.core, self.first))

    def swap(self, k, group):
        self.swaps.append(
            send(group, group, self.swap_s.at[k], self.swap_r.at[k], "seq", self.partner)
        )

    def cross(self):
        for k in ARRIVAL:
            for i in range(SIDE):
                self.far[i, k].wait_recv()
            self.swap(k + 1, self.view(self.core, (self.first + SIDE - 1 - k) % SIDE))

    def finish(self):
        for copy in self.swaps:
            copy.wait_recv()

    def drain(self):
        for copy in self.near + list(self.far.values()) + self.swaps:
            copy.wait_send()


def step_kernel(
    context_hbm, owner_hbm, index_hbm, lens_hbm, states_hbm, gain_hbm, w_hbm, w_out_hbm,
    frequency_hbm, cache_hbm,
    hidden_ref, rows_ref,
    context_ref, owner_ref, index_ref, lens_ref, states_ref, gain_ref, w_ref, w_out_ref,
    frequency_ref, cache, scaled, own, snd0, rcv0, snd1, rcv1, snd2, rcv2, query_pool, fresh_pool, query_rows,
    scores, pool, terms, arrived,
    sem_in, sem0s, sem0r, sem1s, sem1r, sem2s, sem2r,
    q0, q1, q2, q3, q4, q5, k0, k1, k2, k3, k4, k5, o0, o1, o2, o3, o4, o5, sem4s, sem4r,
):
    where = place()
    core, first, second, partner, primary, secondary = where
    tp = lax.axis_index("tp")
    sides = [(tp + i) % SIDE for i in range(1, SIDE)]
    greet("seq", [partner] + primary + secondary)
    greet("tp", sides)
    loads = {}
    for i, (name, source, target) in enumerate(
        (
            ("states", states_hbm, states_ref), ("gain", gain_hbm, gain_ref),
            ("w", w_hbm, w_ref), ("context", context_hbm, context_ref),
            ("owner", owner_hbm, owner_ref), ("index", index_hbm, index_ref),
            ("lens", lens_hbm, lens_ref), ("frequency", frequency_hbm, frequency_ref),
            ("w_out", w_out_hbm, w_out_ref), ("cache", cache_hbm, cache),
        )
    ):
        loads[name] = pltpu.make_async_copy(source, target, sem_in.at[i])
        loads[name].start()

    parts, _, columns = w_ref.shape
    width = parts * columns
    blocks, _, tokens, _ = cache.shape
    heads = columns // HEAD_DIM
    requests = context_ref.shape[0]
    half_rows = requests // 2

    loads["states"].wait()
    loads["gain"].wait()
    states = states_ref[...].astype(jnp.float32).T
    scaled[...] = (states * gain_ref[...].astype(jnp.float32)).astype(jnp.bfloat16)
    squares = jnp.sum(states * states, axis=1, keepdims=True)
    squares = jnp.broadcast_to(squares, (requests, LANES))
    squares = [squares[:half_rows], squares[half_rows:]]
    shape = (SIDE, SIDE, GROUP)
    loads["w"].wait()
    rows = scaled[pl.ds(pl.multiple_of((1 - core) * half_rows, half_rows), half_rows), :]
    for part in range(parts):
        term = jnp.dot(rows, w_ref[part], preferred_element_type=jnp.float32)
        snd0[:, :, :, part * columns : (part + 1) * columns] = term.reshape(
            shape + (columns,)
        ).astype(jnp.bfloat16)
    snd0[:, :, :, width:] = halves(jnp.where(core == 0, squares[1], squares[0])).reshape(
        shape + (LANES,)
    )
    pl.semaphore_wait(pltpu.get_barrier_semaphore(), 10)
    copies0 = {}
    for i in ORDER + (0,):
        chunk = (second + i) % SIDE
        copies0[i] = send(
            snd0.at[chunk], rcv0.at[chunk], sem0s.at[i], sem0r.at[i], "seq", partner
        )
    rows = scaled[pl.ds(pl.multiple_of(core * half_rows, half_rows), half_rows), :]
    for part in range(parts):
        term = jnp.dot(rows, w_ref[part], preferred_element_type=jnp.float32)
        own[:, :, :, part * columns : (part + 1) * columns] = term.reshape(shape + (columns,))
    own[:, :, :, width:] = jnp.where(core == 0, squares[0], squares[1]).reshape(shape + (LANES,))

    copies1 = {}
    for i in ORDER:
        copies0[i].wait_recv()
        a = (first + i) % SIDE
        for j in ORDER + (0,):
            b = (second + j) % SIDE
            snd1[i - 1, j, :, :width] = (
                own[a, b, :, :width] + rcv0[a, b, :, :width].astype(jnp.float32)
            ).astype(jnp.bfloat16)
            snd1[i - 1, j, :, width:] = halves(own[a, b, :, width:] + whole(rcv0[a, b, :, width:]))
            copies1[i, j] = send(
                snd1.at[i - 1, j], rcv1.at[i - 1, j], sem1s.at[i - 1, j], sem1r.at[i - 1, j],
                "seq", primary[i - 1],
            )

    for name in ("context", "owner", "index", "lens", "frequency", "w_out"):
        loads[name].wait()
    here = (core * SIDE + first) * SIDE + second
    row = lax.broadcasted_iota(jnp.int32, (GROUP, columns), 0)
    position = jnp.zeros((GROUP, columns), jnp.int32)
    for i in range(GROUP):
        position = jnp.where(row == i, context_ref[here * GROUP + i] - 1, position)
    angle = position.astype(jnp.float32) * frequency_ref[...]
    cosine = jnp.cos(angle)
    is_front = lax.broadcasted_iota(jnp.int32, (GROUP, columns), 1) % HEAD_DIM < HEAD_DIM // 2
    sine = jnp.sin(angle)
    sine = jnp.where(is_front, -sine, sine)
    slot = lax.broadcasted_iota(jnp.int32, (blocks, requests), 0)
    wanted = jnp.zeros((blocks, requests), jnp.int32)
    lane = lax.broadcasted_iota(jnp.int32, (heads, LANES), 1)
    owner_lanes = jnp.full((heads, LANES), requests, jnp.int32)
    owners, seen, targets = [], [], []
    for j in range(blocks):
        owner = owner_ref[j]
        live = owner < requests
        last = context_ref[jnp.minimum(owner, requests - 1)] - 1
        hit = live & (index_ref[j] == last // tokens)
        wanted = jnp.where(slot == j, owner, wanted)
        owner_lanes = jnp.where(lane == j, owner, owner_lanes)
        owners.append(owner)
        seen.append(jnp.where(live, last + 1 - index_ref[j] * tokens, 0))
        targets.append(jnp.where(hit, last % tokens, -1))
    pick = jnp.where(
        lax.broadcasted_iota(jnp.int32, (blocks, requests), 1) == wanted, 1.0, 0.0
    ).astype(jnp.bfloat16)
    head_mask = (
        lax.broadcasted_iota(jnp.int32, (heads, columns), 1) // HEAD_DIM
        == lax.broadcasted_iota(jnp.int32, (heads, columns), 0)
    )
    pool[:, :, :, blocks:, :] = jnp.zeros(
        (2, SIDE, SIDE, pool.shape[3] - blocks, pool.shape[4]), jnp.bfloat16
    )
    lens = lens_ref[...]
    ids = lax.broadcasted_iota(jnp.int32, lens.shape, 0) * lens.shape[1] + (
        lax.broadcasted_iota(jnp.int32, lens.shape, 1)
    )
    candidates = jnp.where(lens > LONG_LIMIT, ids, -1).astype(jnp.float32)
    long_ids = []
    for _ in range(LONG_REQS):
        top = jnp.max(jnp.max(candidates, axis=1, keepdims=True), axis=0, keepdims=True)
        long_ids.append(top)
        candidates = jnp.where(candidates == top, -1.0, candidates)

    copies0[0].wait_recv()
    copies2 = {}
    for j in ORDER + (0,):
        b = (second + j) % SIDE
        term = own[first, b, :, :width] + rcv0[first, b, :, :width].astype(jnp.float32)
        total = own[first, b, :, width:] + whole(rcv0[first, b, :, width:])
        for i in ORDER:
            copies1[i, j].wait_recv()
            term = term + rcv1[i - 1, j, :, :width].astype(jnp.float32)
            total = total + whole(rcv1[i - 1, j, :, width:])
        if j:
            snd2[j - 1, :, :width] = term.astype(jnp.bfloat16)
            snd2[j - 1, :, width:] = halves(total)
            copies2[j] = send(
                snd2.at[j - 1], rcv2.at[j - 1], sem2s.at[j - 1], sem2r.at[j - 1],
                "seq", secondary[j - 1],
            )
    loads["cache"].wait()
    for j in (1, 3, 2):
        copies2[j].wait_recv()
        term = term + rcv2[j - 1, :, :width].astype(jnp.float32)
        total = total + whole(rcv2[j - 1, :, width:])

    inverse = lax.rsqrt(total / (HEAD_DIM * 32) + EPSILON)[:, :1]
    query = rotated(term[:, :columns] * inverse, cosine, sine, is_front) * HEAD_DIM ** (-0.5)
    query_pool[core, first, second] = query.astype(jnp.bfloat16)
    queries = Gather(query_pool, (q0, q1, q2, q3, q4, q5), where)
    queries.start()
    key = rotated(term[:, columns : 2 * columns] * inverse, cosine, sine, is_front)
    fresh_pool[core, first, second, :, :columns] = key.astype(jnp.bfloat16)
    fresh_pool[core, first, second, :, columns:] = (term[:, 2 * columns :] * inverse).astype(
        jnp.bfloat16
    )
    news = Gather(fresh_pool, (k0, k1, k2, k3, k4, k5), where)
    news.start()
    queries.relay()
    news.relay()
    queries.cross()
    queries.finish()

    def picked(piece):
        piece = piece.astype(jnp.float32).reshape(requests, columns).astype(jnp.bfloat16)
        return jnp.dot(pick, piece, preferred_element_type=jnp.float32)

    query_rows[...] = picked(query_pool[...])
    for j in range(blocks):
        if j == blocks // 2:
            news.cross()
        spread = jnp.where(head_mask, query_rows[j : j + 1, :], 0.0).astype(jnp.bfloat16)
        scores[j] = lax.dot_general(
            spread, cache[j, 0], (((1,), (1,)), ((), ())), preferred_element_type=jnp.float32
        )
    news.finish()
    key_rows = picked(fresh_pool[:, :, :, :, :columns])
    value_rows = picked(fresh_pool[:, :, :, :, columns:])
    product = query_rows[...] * key_rows
    high = product.astype(jnp.bfloat16)
    low = (product - high.astype(jnp.float32)).astype(jnp.bfloat16)
    head_rows = jnp.where(head_mask, 1.0, 0.0).astype(jnp.bfloat16)
    new_scores = sum(
        lax.dot_general(
            head_rows, piece, (((1,), (1,)), ((), ())), preferred_element_type=jnp.float32
        )
        for piece in (high, low)
    )

    token = lax.broadcasted_iota(jnp.int32, (heads, tokens), 1)
    masked = []
    peaks = jnp.full((heads, LANES), NEG_FLOOR, jnp.float32)
    for j in range(blocks):
        value = jnp.where(token == targets[j], new_scores[:, j : j + 1], scores[j])
        value = jnp.where(token < seen[j], value, NEG_FLOOR)
        masked.append(value)
        peaks = jnp.where(lane == j, jnp.max(value, axis=1, keepdims=True), peaks)
    group_peaks = jnp.zeros((heads, LANES), jnp.float32)
    sums = jnp.zeros((heads, LANES), jnp.float32)
    weights, new_weights = [], []
    for j in range(blocks):
        same = owner_lanes == owners[j]
        peak = jnp.max(jnp.where(same, peaks, NEG_FLOOR), axis=1, keepdims=True)
        weight = jnp.where(token < seen[j], jnp.exp(masked[j] - peak), 0.0)
        weight = weight.astype(jnp.bfloat16).astype(jnp.float32)
        is_new = token == targets[j]
        weights.append(jnp.where(is_new, 0.0, weight).astype(jnp.bfloat16))
        new_weights.append(jnp.sum(jnp.where(is_new, weight, 0.0), axis=1, keepdims=True))
        group_peaks = jnp.where(lane == j, peak, group_peaks)
        sums = jnp.where(lane == j, jnp.sum(weight, axis=1, keepdims=True), sums)
    group_sums = jnp.zeros((heads, LANES), jnp.float32)
    leads = jnp.zeros((heads, LANES), jnp.float32)
    lines = []
    for j in range(blocks):
        same = owner_lanes == owners[j]
        total = jnp.sum(jnp.where(same, sums, 0.0), axis=1, keepdims=True)
        group_sums = jnp.where(lane == j, total, group_sums)
        earlier = jnp.max(jnp.where(same & (lane < j), 1.0, 0.0), axis=1, keepdims=True)
        leads = jnp.where(lane == j, 1.0 - earlier, leads)
        inverse = jnp.where(total > 0.0, 1.0 / jnp.where(total > 0.0, total, 1.0), 0.0)
        piece = jnp.dot(weights[j], cache[j, 1], preferred_element_type=jnp.float32)
        piece = piece + new_weights[j] * value_rows[j : j + 1]
        piece = jnp.where(head_mask, piece * inverse, 0.0)
        lines.append(jnp.sum(piece, axis=0, keepdims=True))
    for j in range(0, blocks, GROUP):
        pool[core, first, second, j : j + GROUP, :columns] = jnp.concatenate(
            lines[j : j + GROUP], axis=0
        ).astype(jnp.bfloat16)
    quarter = LANES // 4
    stats = group_peaks
    for f, field in enumerate((group_sums, leads, owner_lanes.astype(jnp.float32))):
        stats = jnp.where(lane // quarter == f + 1, pltpu.roll(field, (f + 1) * quarter, 1), stats)
    for j in range(0, blocks, GROUP):
        piece = stats.astype(jnp.bfloat16)
        pool[core, first, second, j : j + GROUP, columns:] = piece
        stats = stats - piece.astype(jnp.float32)
    outputs = Gather(pool, (o0, o1, o2, o3, o4, o5), where, blocks)
    outputs.start()
    outputs.relay()

    rows_ref[:, :columns] = key_rows.astype(jnp.bfloat16)
    rows_ref[:, columns:] = value_rows.astype(jnp.bfloat16)
    outputs.cross()
    outputs.finish()

    devices = 2 * SIDE * SIDE
    fields = [[] for _ in range(4)]
    for start in range(0, devices, 4):
        tiles = []
        for d in range(start, start + 4):
            tile = pool[
                d // (SIDE * SIDE), d // SIDE % SIDE, d % SIDE, :, columns:
            ].astype(jnp.float32)
            tiles.append(tile[:8] + tile[8:16] + tile[16:24])
        for f in range(4):
            merged = jnp.zeros((heads, LANES), jnp.float32)
            for k in range(4):
                shift = (k - f) * quarter % LANES
                tile = tiles[k] if shift == 0 else pltpu.roll(tiles[k], shift, 1)
                merged = jnp.where(lane // quarter == k, tile, merged)
            fields[f].append(merged)
    peaks, sums, leads, slot_owners = [jnp.concatenate(f, axis=1) for f in fields]
    used = lax.broadcasted_iota(jnp.int32, slot_owners.shape, 1) % quarter < blocks
    slot_owners = jnp.where(used, slot_owners, float(requests))
    high_rows, low_rows = [], []
    is_long = jnp.zeros(slot_owners.shape, jnp.bool_)
    for long_id in long_ids:
        match = slot_owners == long_id
        is_long = is_long | match
        peak = jnp.max(jnp.where(match, peaks, NEG_FLOOR), axis=1, keepdims=True)
        mass = jnp.where(match, sums * jnp.exp(jnp.where(match, peaks, NEG_FLOOR) - peak), 0.0)
        weight = mass / jnp.sum(jnp.where(match, mass * leads, 0.0), axis=1, keepdims=True)
        high = weight.astype(jnp.bfloat16).astype(jnp.float32)
        high_rows.append(high)
        low_rows.append(weight - high)
    request = lax.broadcasted_iota(jnp.int32, (requests, devices * quarter), 0)
    short_owner = jnp.where(is_long, float(requests), slot_owners)[:1]
    member = jnp.where(request.astype(jnp.float32) == short_owner, 1.0, 0.0).astype(jnp.bfloat16)
    extra = jnp.concatenate(high_rows + low_rows, axis=0).astype(jnp.bfloat16)
    values = pool[:, :, :, :, :columns].reshape(devices * quarter, columns)
    attended = jnp.dot(member, values, preferred_element_type=jnp.float32)
    weighted = jnp.dot(extra, values, preferred_element_type=jnp.float32)
    row = lax.broadcasted_iota(jnp.int32, (requests, 1), 0).astype(jnp.float32)
    half = LONG_REQS * heads
    for l, long_id in enumerate(long_ids):
        both = weighted[l * heads : (l + 1) * heads] + weighted[
            half + l * heads : half + (l + 1) * heads
        ]
        line = jnp.sum(jnp.where(head_mask, both, 0.0), axis=0, keepdims=True)
        attended = jnp.where(row == long_id, line, attended)
    result = lax.dot_general(
        attended.astype(jnp.bfloat16), w_out_ref[...], (((1,), (1,)), ((), ())),
        preferred_element_type=jnp.float32,
    )
    share = requests // SIDE
    terms[...] = result.reshape(SIDE, share, result.shape[1])
    copies = [
        send(terms.at[sides[i]], arrived.at[i], sem4s.at[i], sem4r.at[i], "tp", sides[i])
        for i in range(SIDE - 1)
    ]
    pairs = [
        states_ref[:, i * LANES : (i + 1) * LANES].astype(jnp.float32).T
        for i in range(requests // LANES)
    ]
    pair = jnp.where(tp // 2 == 0, pairs[0], pairs[1])
    total = terms[tp] + jnp.where(tp % 2 == 0, pair[:share], pair[share:])
    for copy in copies:
        copy.wait_recv()
    for i in range(SIDE - 1):
        total = total + arrived[i]
    hidden_ref[...] = total.astype(jnp.bfloat16)
    for group in (copies0, copies1, copies2):
        for copy in group.values():
            copy.wait_send()
    for gather in (queries, news, outputs):
        gather.drain()
    for copy in copies:
        copy.wait_send()


def store_kernel(
    context_ref, owner_ref, index_ref, hidden_in_ref, rows_ref, cache_ref,
    hidden_ref, updated_ref, changed, sem,
):
    hidden_ref[...] = hidden_in_ref[...]
    blocks, _, tokens, columns = updated_ref.shape
    requests = context_ref.shape[0]
    groups = tokens // ROW_GROUP
    row = lax.broadcasted_iota(jnp.int32, (ROW_GROUP, columns), 0)
    for j in range(blocks):
        owner = owner_ref[j]
        last = context_ref[jnp.minimum(owner, requests - 1)] - 1
        hit = (owner < requests) & (index_ref[j] == last // tokens)
        place_in = last % tokens

        @pl.when(hit)
        def _(j=j, place_in=place_in):
            group = place_in // ROW_GROUP
            base = pl.multiple_of(group * ROW_GROUP, ROW_GROUP)
            for i in range(1, groups):
                at = pl.ds(pl.multiple_of((group + i) % groups * ROW_GROUP, ROW_GROUP), ROW_GROUP)
                pltpu.make_async_copy(
                    cache_ref.at[j, :, at], updated_ref.at[j, :, at], sem.at[j]
                ).start()
            for c in range(2):
                fresh = rows_ref[j : j + 1, c * columns : (c + 1) * columns]
                old = cache_ref[j, c, pl.ds(base, ROW_GROUP), :]
                changed[j, c] = jnp.where(
                    row == place_in - base, fresh.astype(jnp.float32), old.astype(jnp.float32)
                ).astype(jnp.bfloat16)
            pltpu.make_async_copy(
                changed.at[j], updated_ref.at[j, :, pl.ds(base, ROW_GROUP)], sem.at[j]
            ).start()

        @pl.when(jnp.logical_not(hit))
        def _(j=j):
            pltpu.make_async_copy(cache_ref.at[j], updated_ref.at[j], sem.at[j]).start()

    for j in range(blocks):
        pltpu.make_async_copy(cache_ref.at[j], updated_ref.at[j], sem.at[j]).wait()


def shards(states, norm_gain, w_qkv, w_out, cache, context_len, block_owner, block_index):
    requests, depth = states.shape
    parts, _, columns = w_qkv.shape
    width = parts * columns
    wide = width + LANES
    blocks = cache.shape[0]
    heads = columns // HEAD_DIM
    half_dim = HEAD_DIM // 2
    base = 10000.0 ** (-np.arange(half_dim, dtype=np.float64) * 2.0 / HEAD_DIM)
    frequency = jnp.asarray(np.tile(base, 2 * heads).astype(np.float32)[None, :])
    vmem = pl.BlockSpec(memory_space=pltpu.VMEM)
    smem = pl.BlockSpec(memory_space=pltpu.SMEM)
    hbm = pl.BlockSpec(memory_space=pltpu.HBM)
    dma = pltpu.SemaphoreType.DMA
    bf16 = jnp.bfloat16
    f32 = jnp.float32
    n = SIDE - 1
    share = requests // SIDE
    gather_sems = [dma((n,)), dma((n,)), dma((SIDE, n)), dma((SIDE, n)), dma((SIDE,)), dma((SIDE,))]
    hidden, rows = pl.pallas_call(
        step_kernel,
        name="step",
        out_shape=(
            jax.ShapeDtypeStruct((share, depth), bf16),
            jax.ShapeDtypeStruct((blocks, 2 * columns), bf16),
        ),
        in_specs=[hbm] * 10,
        out_specs=(vmem, vmem),
        scratch_shapes=[
            pltpu.SMEM((requests,), jnp.int32),
            pltpu.SMEM((blocks,), jnp.int32),
            pltpu.SMEM((blocks,), jnp.int32),
            pltpu.VMEM((2, requests // 2), jnp.int32),
            pltpu.VMEM((depth, requests), bf16),
            pltpu.VMEM((1, depth), bf16),
            pltpu.VMEM(w_qkv.shape, bf16),
            pltpu.VMEM((depth, columns), bf16),
            pltpu.VMEM((1, columns), f32),
            pltpu.VMEM(cache.shape, bf16),
            pltpu.VMEM((requests, depth), bf16),
            pltpu.VMEM((SIDE, SIDE, GROUP, wide), f32),
            pltpu.VMEM((SIDE, SIDE, GROUP, wide), bf16),
            pltpu.VMEM((SIDE, SIDE, GROUP, wide), bf16),
            pltpu.VMEM((n, SIDE, GROUP, wide), bf16),
            pltpu.VMEM((n, SIDE, GROUP, wide), bf16),
            pltpu.VMEM((n, GROUP, wide), bf16),
            pltpu.VMEM((n, GROUP, wide), bf16),
            pltpu.VMEM((2, SIDE, SIDE, GROUP, columns), bf16),
            pltpu.VMEM((2, SIDE, SIDE, GROUP, 2 * columns), bf16),
            pltpu.VMEM((blocks, columns), f32),
            pltpu.VMEM((blocks, heads, cache.shape[2]), f32),
            pltpu.VMEM((2, SIDE, SIDE, LANES // 4, columns + LANES), bf16),
            pltpu.VMEM((SIDE, share, depth), f32),
            pltpu.VMEM((n, share, depth), f32),
            dma((10,)),
            dma((SIDE,)), dma((SIDE,)),
            dma((n, SIDE)), dma((n, SIDE)),
            dma((n,)), dma((n,)),
        ]
        + gather_sems * 3
        + [dma((n,)), dma((n,))],
        compiler_params=pltpu.CompilerParams(
            collective_id=0, has_side_effects=True, vmem_limit_bytes=32 << 20
        ),
        cost_estimate=pl.CostEstimate(
            flops=10**9, bytes_accessed=cache.size * 2, transcendentals=10**5
        ),
    )(
        *(
            pltpu.with_memory_space_constraint(array, pltpu.HBM)
            for array in (
                context_len, block_owner, block_index, context_len.reshape(2, requests // 2),
                states.T, norm_gain[None, :], w_qkv, w_out.T, frequency, cache,
            )
        )
    )
    return pl.pallas_call(
        store_kernel,
        name="store",
        out_shape=(
            jax.ShapeDtypeStruct(hidden.shape, bf16),
            jax.ShapeDtypeStruct(cache.shape, bf16),
        ),
        in_specs=[smem, smem, smem, vmem, vmem, vmem],
        out_specs=(vmem, hbm),
        scratch_shapes=[pltpu.VMEM((blocks, 2, ROW_GROUP, columns), bf16), dma((blocks,))],
        compiler_params=pltpu.CompilerParams(vmem_limit_bytes=16 << 20),
    )(context_len, block_owner, block_index, hidden, rows, cache)


def solution(mesh):
    return jax.shard_map(
        shards,
        mesh=mesh,
        in_specs=(
            P(None, "seq"),
            P("seq"),
            P(None, "seq", "tp"),
            P("tp", "seq"),
            P("seq", None, None, "tp"),
            P(),
            P("seq"),
            P("seq"),
        ),
        out_specs=(P("tp", "seq"), P("seq", None, None, "tp")),
        check_vma=False,
    )
```

time: 402 us -> 52.1 us (0.13)
  waiting for transfers between devices: 168 us -> 0 us
  blocking collectives: 113 us -> 0 us
  local copies, waits for them, and re-layouts: 71.3 us -> 0.02 us
  Pallas kernels: 0 us -> 51.3 us
  other arithmetic: 18 us -> 0 us
  between operations: 14.1 us -> 0.7 us
  matrix products: 11.8 us -> 0 us
    psum x1 -> x0, waiting for transfers between devices: 106 us -> none  [shards(): projected = lax.psum(local_term, 'seq')]
    psum x1 -> x0, blocking collectives: 65.1 us -> none  [shards(): sum_squares = lax.psum(jnp.sum(wide_states * wide_states, axis=1), 'seq')]
    pallas_call x0 -> x2, Pallas kernels: none -> 51.3 us  [the longest x1 47.8 us: shards(): pl.pallas_call(step_kernel, name='step', out_shape=(jax.ShapeDtypeStruct(...]
    all_gather x2 -> x0, blocking collectives: 48.1 us -> none  [combined_all(): gathered = jax.tree.map(lambda a: lax.all_gather(a, axis), part)]
    dynamic_slice x65 -> x0, local copies, waits for them, and re-layouts: 46.3 us -> none  [take(): lax.dynamic_index_in_dim(a, source, 0, False)]
    all_gather x1 -> x0, waiting for transfers between devices: 44.9 us -> none  [combined_all(): gathered = jax.tree.map(lambda a: lax.all_gather(a, axis), part)]
    unnamed x4 -> x0, waiting for transfers between devices: 17.1 us -> none
    dot_general x5 -> x0, matrix products: 10.9 us -> none  [the longest x1 3.6 us: shards(): jnp.einsum('bhd,bthd->bht', query_rows, key_cache, preferred_element_type...]
  transfers between devices with their start and end apart: 3 -> 0, of which waited for: 3 -> 0; matrix products, arithmetic and copies ran while one was open for 1% -> 0% of each run, Pallas kernels for 0% -> 0%
where the time goes in v2:
time: 52.1 us; the launch traced here: 52 us
  Pallas kernels  51.3 us (98%)
  between operations  0.7 us (1%)
    pallas_call x1, Pallas kernels, shards(): pl.pallas_call(step_kernel, name='step', out_shape=(jax.ShapeDtypeStruct(...  47.8 us
    pallas_call x1, Pallas kernels, shards(): pl.pallas_call(store_kernel, name='store', out_shape=(jax.ShapeDtypeStruc...  3.53 us

profile of v2, /device:TPU:1, one launch (start us, length us, event | category | flops | bytes accessed | tf_op | source)
XLA Modules:
  0.0 52.0 jit_solution(8953925679263588365)
XLA Ops:
  0.6 0.0 copy-start.1
  0.6 0.0 copy-start.3
  0.7 0.0 copy-start.2
  0.7 0.0 copy-start
  0.7 47.8 %step.1 = (bf16[64,96]{1,0:T(8,128)(2,1)S(1)}, bf16[24,1536]{1,0:T(8,128)(2,1)S(1)}) custom-call(s32[256]{0:T(256)} %context_ref.1, s32[24]{0:T(128)} %owner_ref.1, s32[24]{0:T(128)} %index_ref.1, s32[2,128]{1,0:T(2,128)} %bitcast.4, bf16[96,256]{1,0:T(8,128)(2,1)} %bitcast.6, bf16[1,96]{1,0:T(2,128)(2,1)} %bitcast.7, bf16[3,96,768]{2,1,0:T(8,128)(2,1)} %w_hbm.1, ...), custom_call_target="tpu_custom_call" | custom-call | flops 1000000000 | bytes 4718592 | tf_op jit(solution)/shard_map/step/pallas_call | solution.py:529
  48.4 0.0 copy-done.1
  48.5 0.0 copy-done.3
  48.5 0.0 copy-done.2
  48.5 0.0 copy-done
  48.5 3.5 %store.1 = (bf16[64,96]{1,0:T(8,128)(2,1)}, bf16[24,2,64,768]{3,2,1,0:T(8,128)(2,1)}) custom-call(s32[256]{0:T(256)S(1)} %copy-done.1, s32[24]{0:T(128)S(1)} %copy-done.2, s32[24]{0:T(128)S(1)} %copy-done.3, bf16[64,96]{1,0:T(8,128)(2,1)S(1)} %get-tuple-element.4.hidden_in_ref, bf16[24,1536]{1,0:T(8,128)(2,1)S(1)} %get-tuple-element.5.rows_ref, ...), custom_call_target="tpu_custom_call" | custom-call | tf_op jit(solution)/shard_map/store/pallas_call | solution.py:586
Async XLA Ops:
  0.6 47.8 %copy-start.1 = (s32[256]{0:T(256)S(1)}, s32[256]{0:T(256)}, u32[]{:S(2)}) copy-start(s32[256]{0:T(256)} %context_ref.1) | copy-start | bytes 3076
  0.6 47.8 %copy-start.3 = (s32[24]{0:T(128)S(1)}, s32[24]{0:T(128)}, u32[]{:S(2)}) copy-start(s32[24]{0:T(128)} %index_ref.1) | copy-start | bytes 292
  0.7 47.8 %copy-start.2 = (s32[24]{0:T(128)S(1)}, s32[24]{0:T(128)}, u32[]{:S(2)}) copy-start(s32[24]{0:T(128)} %owner_ref.1) | copy-start | bytes 292
  0.7 47.8 %copy-start = (bf16[24,2,64,768]{3,2,1,0:T(8,128)(2,1)S(1)}, bf16[24,2,64,768]{3,2,1,0:T(8,128)(2,1)}, u32[]{:S(2)}) copy-start(bf16[24,2,64,768]{3,2,1,0:T(8,128)(2,1)} %cache_ref.1) | copy-start | bytes 14155780

commit v3 on v2

--- a/solution.py
+++ b/solution.py
@@ -17,6 +17,7 @@
 LONG_LIMIT = 31 * 64
 LONG_REQS = 4
 ORDER = (2, 1, 3)
+DEPARTURE = (1, 0, 2)
 ARRIVAL = (0, 2, 1)
 ROW_GROUP = 16
 
@@ -34,10 +35,16 @@
         yy = b * (1 - core) + a * core
         return (zz * SIDE + yy) * 2 + core
 
-    primary = [device((first + i) % SIDE, second) for i in range(1, SIDE)]
-    secondary = [device(first, (second + i) % SIDE) for i in range(1, SIDE)]
+    peers = {
+        (i, j): device((first + i) % SIDE, (second + j) % SIDE)
+        for i in range(SIDE)
+        for j in range(SIDE)
+        if (i, j) != (0, 0)
+    }
+    primary = [peers[i, 0] for i in range(1, SIDE)]
+    secondary = [peers[0, j] for j in range(1, SIDE)]
     partner = me + 1 - 2 * core
-    return core, first, second, partner, primary, secondary
+    return core, first, second, partner, primary, secondary, peers
 
 
 def send(src, dst, send_sem, recv_sem, axis, to):
@@ -81,10 +88,85 @@
     return values * cosine + other * sine
 
 
+class Reduce:
+    def __init__(self, refs, sems, where, squares):
+        self.own, self.snd0, self.rcv0, self.snd1, self.rcv1, self.snd2, self.rcv2 = refs
+        self.sems = sems
+        self.first, self.second, self.partner, self.primary, self.secondary = where[1:6]
+        self.squares = squares
+        self.width = self.own.shape[-1] - (LANES if squares else 0)
+        self.copies = []
+
+    def put(self, ref, index, body, total):
+        ref[index + (slice(None), slice(0, self.width))] = body.astype(jnp.bfloat16)
+        if self.squares:
+            ref[index + (slice(None), slice(self.width, None))] = halves(total)
+
+    def add(self, term, ref, index):
+        body, total = term
+        body = body + ref[index + (slice(None), slice(0, self.width))].astype(jnp.float32)
+        if self.squares:
+            total = total + whole(ref[index + (slice(None), slice(self.width, None))])
+        return body, total
+
+    def local(self, a, b):
+        total = self.own[a, b, :, self.width :] if self.squares else None
+        return self.add((self.own[a, b, :, : self.width], total), self.rcv0, (a, b))
+
+    def send(self, src, dst, stage, index, to):
+        copy = send(
+            src, dst, self.sems[2 * stage].at[index], self.sems[2 * stage + 1].at[index], "seq", to
+        )
+        self.copies.append(copy)
+        return copy
+
+    def swap(self):
+        self.swapped = {}
+        for i in ORDER + (0,):
+            b = (self.first + i) % SIDE
+            self.swapped[i] = self.send(self.snd0.at[:, b], self.rcv0.at[:, b], 0, i, self.partner)
+
+    def begin(self):
+        self.across = {}
+        for j in ORDER + (0,):
+            self.swapped[j].wait_recv()
+            b = (self.second + j) % SIDE
+            for i in ORDER:
+                self.put(self.snd1, (i - 1, j), *self.local((self.first + i) % SIDE, b))
+                self.across[i, j] = self.send(
+                    self.snd1.at[i - 1, j], self.rcv1.at[i - 1, j], 1, (i - 1, j),
+                    self.primary[i - 1],
+                )
+
+    def middle(self):
+        self.along = {}
+        for j in ORDER + (0,):
+            term = self.local(self.first, (self.second + j) % SIDE)
+            for i in ORDER:
+                self.across[i, j].wait_recv()
+                term = self.add(term, self.rcv1, (i - 1, j))
+            if j:
+                self.put(self.snd2, (j - 1,), *term)
+                self.along[j] = self.send(
+                    self.snd2.at[j - 1], self.rcv2.at[j - 1], 2, j - 1, self.secondary[j - 1]
+                )
+        self.term = term
+
+    def end(self):
+        for j in (1, 3, 2):
+            self.along[j].wait_recv()
+            self.term = self.add(self.term, self.rcv2, (j - 1,))
+        return self.term
+
+    def drain(self):
+        for copy in self.copies:
+            copy.wait_send()
+
+
 class Gather:
     def __init__(self, ref, sems, where, part=None):
         self.ref, self.part = ref, part
-        self.core, self.first, self.second, self.partner, self.primary, self.secondary = where
+        self.core, self.first, self.second, self.partner, self.primary, self.secondary, _ = where
         self.near_s, self.near_r, self.far_s, self.far_r, self.swap_s, self.swap_r = sems
         self.far = {}
         self.swaps = []
@@ -96,17 +178,17 @@
         return self.ref.at[index + fill + (pl.ds(0, self.part),)]
 
     def forward(self, i, block):
-        for k in range(SIDE - 1):
+        for k in DEPARTURE:
             self.far[i, k] = send(
                 block, block, self.far_s.at[i, k], self.far_r.at[i, k], "seq", self.primary[k]
             )
 
     def start(self):
         block = self.view(self.core, self.first, self.second)
-        self.near = [
-            send(block, block, self.near_s.at[i], self.near_r.at[i], "seq", self.secondary[i])
-            for i in range(SIDE - 1)
-        ]
+        self.near = {
+            i: send(block, block, self.near_s.at[i], self.near_r.at[i], "seq", self.secondary[i])
+            for i in DEPARTURE
+        }
         self.forward(0, block)
 
     def relay(self):
@@ -134,8 +216,54 @@
             copy.wait_recv()
 
     def drain(self):
-        for copy in self.near + list(self.far.values()) + self.swaps:
+        for copy in list(self.near.values()) + list(self.far.values()) + self.swaps:
             copy.wait_send()
+
+
+class Direct:
+    def __init__(self, ref, sems, where):
+        self.ref = ref
+        self.core, self.first, _, self.partner, _, _, self.peers = where
+        self.send_sem, self.recv_sem, self.swap_s, self.swap_r = sems
+        self.second = where[2]
+        self.swaps = []
+
+    def start(self):
+        block = self.ref.at[self.core, self.first, self.second]
+        far = lambda at: min(at[0], SIDE - at[0]) + min(at[1], SIDE - at[1])
+        self.copies = {
+            at: send(
+                block, block, self.send_sem.at[at], self.recv_sem.at[at], "seq", self.peers[at]
+            )
+            for at in sorted(self.peers, key=far, reverse=True)
+        }
+
+    def cross(self, groups):
+        for i in groups:
+            for j in range(SIDE):
+                if (i, j) != (0, 0):
+                    self.copies[i, j].wait_recv()
+            group = self.ref.at[self.core, (self.first + SIDE - i) % SIDE]
+            self.swaps.append(
+                send(group, group, self.swap_s.at[i], self.swap_r.at[i], "seq", self.partner)
+            )
+
+    def finish(self):
+        for copy in self.swaps:
+            copy.wait_recv()
+
+    def drain(self):
+        for copy in list(self.copies.values()) + self.swaps:
+            copy.wait_send()
+
+
+def thirds(value):
+    pieces = []
+    for _ in range(3):
+        piece = value.astype(jnp.bfloat16).astype(jnp.float32)
+        pieces.append(piece)
+        value = value - piece
+    return jnp.concatenate(pieces, axis=0)
 
 
 def step_kernel(
@@ -143,16 +271,16 @@
     frequency_hbm, cache_hbm,
     hidden_ref, rows_ref,
     context_ref, owner_ref, index_ref, lens_ref, states_ref, gain_ref, w_ref, w_out_ref,
-    frequency_ref, cache, scaled, own, snd0, rcv0, snd1, rcv1, snd2, rcv2, query_pool, fresh_pool, query_rows,
-    scores, pool, terms, arrived,
-    sem_in, sem0s, sem0r, sem1s, sem1r, sem2s, sem2r,
-    q0, q1, q2, q3, q4, q5, k0, k1, k2, k3, k4, k5, o0, o1, o2, o3, o4, o5, sem4s, sem4r,
+    frequency_ref, cache, scaled, a0, a1, a2, a3, a4, a5, a6, b0, b1, b2, b3, b4, b5, b6, query_pool, fresh_pool, query_rows,
+    scores, pool, exact, terms, arrived,
+    sem_in, c0, c1, c2, c3, c4, c5, d0, d1, d2, d3, d4, d5,
+    q0, q1, q2, q3, k0, k1, k2, k3, k4, k5, o0, o1, o2, o3, o4, o5, sem4s, sem4r,
 ):
     where = place()
-    core, first, second, partner, primary, secondary = where
+    core, first, second, partner, primary, secondary, peers = where
     tp = lax.axis_index("tp")
     sides = [(tp + i) % SIDE for i in range(1, SIDE)]
-    greet("seq", [partner] + primary + secondary)
+    greet("seq", [partner] + list(peers.values()))
     greet("tp", sides)
     loads = {}
     for i, (name, source, target) in enumerate(
@@ -168,7 +296,6 @@
         loads[name].start()
 
     parts, _, columns = w_ref.shape
-    width = parts * columns
     blocks, _, tokens, _ = cache.shape
     heads = columns // HEAD_DIM
     requests = context_ref.shape[0]
@@ -183,42 +310,33 @@
     squares = [squares[:half_rows], squares[half_rows:]]
     shape = (SIDE, SIDE, GROUP)
     loads["w"].wait()
-    rows = scaled[pl.ds(pl.multiple_of((1 - core) * half_rows, half_rows), half_rows), :]
-    for part in range(parts):
+    ahead = Reduce((a0, a1, a2, a3, a4, a5, a6), (c0, c1, c2, c3, c4, c5), where, True)
+    behind = Reduce((b0, b1, b2, b3, b4, b5, b6), (d0, d1, d2, d3, d4, d5), where, False)
+
+    def project(ref, side, part, at):
+        rows = scaled[pl.ds(pl.multiple_of(side * half_rows, half_rows), half_rows), :]
         term = jnp.dot(rows, w_ref[part], preferred_element_type=jnp.float32)
-        snd0[:, :, :, part * columns : (part + 1) * columns] = term.reshape(
+        ref[:, :, :, at * columns : (at + 1) * columns] = term.reshape(
             shape + (columns,)
-        ).astype(jnp.bfloat16)
-    snd0[:, :, :, width:] = halves(jnp.where(core == 0, squares[1], squares[0])).reshape(
+        ).astype(ref.dtype)
+
+    project(ahead.snd0, 1 - core, 0, 0)
+    ahead.snd0[:, :, :, columns:] = halves(
+        jnp.where(core == 0, squares[1], squares[0])
+    ).reshape(shape + (LANES,))
+    pl.semaphore_wait(pltpu.get_barrier_semaphore(), 19)
+    ahead.swap()
+    project(ahead.own, core, 0, 0)
+    ahead.own[:, :, :, columns:] = jnp.where(core == 0, squares[0], squares[1]).reshape(
         shape + (LANES,)
     )
-    pl.semaphore_wait(pltpu.get_barrier_semaphore(), 10)
-    copies0 = {}
-    for i in ORDER + (0,):
-        chunk = (second + i) % SIDE
-        copies0[i] = send(
-            snd0.at[chunk], rcv0.at[chunk], sem0s.at[i], sem0r.at[i], "seq", partner
-        )
-    rows = scaled[pl.ds(pl.multiple_of(core * half_rows, half_rows), half_rows), :]
-    for part in range(parts):
-        term = jnp.dot(rows, w_ref[part], preferred_element_type=jnp.float32)
-        own[:, :, :, part * columns : (part + 1) * columns] = term.reshape(shape + (columns,))
-    own[:, :, :, width:] = jnp.where(core == 0, squares[0], squares[1]).reshape(shape + (LANES,))
-
-    copies1 = {}
-    for i in ORDER:
-        copies0[i].wait_recv()
-        a = (first + i) % SIDE
-        for j in ORDER + (0,):
-            b = (second + j) % SIDE
-            snd1[i - 1, j, :, :width] = (
-                own[a, b, :, :width] + rcv0[a, b, :, :width].astype(jnp.float32)
-            ).astype(jnp.bfloat16)
-            snd1[i - 1, j, :, width:] = halves(own[a, b, :, width:] + whole(rcv0[a, b, :, width:]))
-            copies1[i, j] = send(
-                snd1.at[i - 1, j], rcv1.at[i - 1, j], sem1s.at[i - 1, j], sem1r.at[i - 1, j],
-                "seq", primary[i - 1],
-            )
+    project(behind.snd0, 1 - core, 1, 0)
+    project(behind.snd0, 1 - core, 2, 1)
+    behind.swap()
+    ahead.begin()
+    project(behind.own, core, 1, 0)
+    project(behind.own, core, 2, 1)
+    behind.begin()
 
     for name in ("context", "owner", "index", "lens", "frequency", "w_out"):
         loads[name].wait()
@@ -232,6 +350,7 @@
     is_front = lax.broadcasted_iota(jnp.int32, (GROUP, columns), 1) % HEAD_DIM < HEAD_DIM // 2
     sine = jnp.sin(angle)
     sine = jnp.where(is_front, -sine, sine)
+    ahead.middle()
     slot = lax.broadcasted_iota(jnp.int32, (blocks, requests), 0)
     wanted = jnp.zeros((blocks, requests), jnp.int32)
     lane = lax.broadcasted_iota(jnp.int32, (heads, LANES), 1)
@@ -267,45 +386,26 @@
         top = jnp.max(jnp.max(candidates, axis=1, keepdims=True), axis=0, keepdims=True)
         long_ids.append(top)
         candidates = jnp.where(candidates == top, -1.0, candidates)
-
-    copies0[0].wait_recv()
-    copies2 = {}
-    for j in ORDER + (0,):
-        b = (second + j) % SIDE
-        term = own[first, b, :, :width] + rcv0[first, b, :, :width].astype(jnp.float32)
-        total = own[first, b, :, width:] + whole(rcv0[first, b, :, width:])
-        for i in ORDER:
-            copies1[i, j].wait_recv()
-            term = term + rcv1[i - 1, j, :, :width].astype(jnp.float32)
-            total = total + whole(rcv1[i - 1, j, :, width:])
-        if j:
-            snd2[j - 1, :, :width] = term.astype(jnp.bfloat16)
-            snd2[j - 1, :, width:] = halves(total)
-            copies2[j] = send(
-                snd2.at[j - 1], rcv2.at[j - 1], sem2s.at[j - 1], sem2r.at[j - 1],
-                "seq", secondary[j - 1],
-            )
     loads["cache"].wait()
-    for j in (1, 3, 2):
-        copies2[j].wait_recv()
-        term = term + rcv2[j - 1, :, :width].astype(jnp.float32)
-        total = total + whole(rcv2[j - 1, :, width:])
+    behind.middle()
+    term, total = ahead.end()
 
     inverse = lax.rsqrt(total / (HEAD_DIM * 32) + EPSILON)[:, :1]
-    query = rotated(term[:, :columns] * inverse, cosine, sine, is_front) * HEAD_DIM ** (-0.5)
+    query = rotated(term * inverse, cosine, sine, is_front) * HEAD_DIM ** (-0.5)
     query_pool[core, first, second] = query.astype(jnp.bfloat16)
-    queries = Gather(query_pool, (q0, q1, q2, q3, q4, q5), where)
+    queries = Direct(query_pool, (q0, q1, q2, q3), where)
     queries.start()
-    key = rotated(term[:, columns : 2 * columns] * inverse, cosine, sine, is_front)
+    term, _ = behind.end()
+    key = rotated(term[:, :columns] * inverse, cosine, sine, is_front)
     fresh_pool[core, first, second, :, :columns] = key.astype(jnp.bfloat16)
-    fresh_pool[core, first, second, :, columns:] = (term[:, 2 * columns :] * inverse).astype(
+    fresh_pool[core, first, second, :, columns:] = (term[:, columns:] * inverse).astype(
         jnp.bfloat16
     )
     news = Gather(fresh_pool, (k0, k1, k2, k3, k4, k5), where)
     news.start()
-    queries.relay()
+    queries.cross((0,))
     news.relay()
-    queries.cross()
+    queries.cross((1, 3, 2))
     queries.finish()
 
     def picked(piece):
@@ -314,45 +414,29 @@
 
     query_rows[...] = picked(query_pool[...])
     for j in range(blocks):
-        if j == blocks // 2:
-            news.cross()
         spread = jnp.where(head_mask, query_rows[j : j + 1, :], 0.0).astype(jnp.bfloat16)
         scores[j] = lax.dot_general(
             spread, cache[j, 0], (((1,), (1,)), ((), ())), preferred_element_type=jnp.float32
         )
-    news.finish()
-    key_rows = picked(fresh_pool[:, :, :, :, :columns])
-    value_rows = picked(fresh_pool[:, :, :, :, columns:])
-    product = query_rows[...] * key_rows
-    high = product.astype(jnp.bfloat16)
-    low = (product - high.astype(jnp.float32)).astype(jnp.bfloat16)
-    head_rows = jnp.where(head_mask, 1.0, 0.0).astype(jnp.bfloat16)
-    new_scores = sum(
-        lax.dot_general(
-            head_rows, piece, (((1,), (1,)), ((), ())), preferred_element_type=jnp.float32
-        )
-        for piece in (high, low)
-    )
 
     token = lax.broadcasted_iota(jnp.int32, (heads, tokens), 1)
-    masked = []
+    masked, visible = [], []
     peaks = jnp.full((heads, LANES), NEG_FLOOR, jnp.float32)
     for j in range(blocks):
-        value = jnp.where(token == targets[j], new_scores[:, j : j + 1], scores[j])
-        value = jnp.where(token < seen[j], value, NEG_FLOOR)
+        visible.append((token < seen[j]) & (token != targets[j]))
+        value = jnp.where(visible[j], scores[j], NEG_FLOOR)
         masked.append(value)
         peaks = jnp.where(lane == j, jnp.max(value, axis=1, keepdims=True), peaks)
     group_peaks = jnp.zeros((heads, LANES), jnp.float32)
     sums = jnp.zeros((heads, LANES), jnp.float32)
-    weights, new_weights = [], []
+    weights = []
     for j in range(blocks):
         same = owner_lanes == owners[j]
         peak = jnp.max(jnp.where(same, peaks, NEG_FLOOR), axis=1, keepdims=True)
-        weight = jnp.where(token < seen[j], jnp.exp(masked[j] - peak), 0.0)
-        weight = weight.astype(jnp.bfloat16).astype(jnp.float32)
-        is_new = token == targets[j]
-        weights.append(jnp.where(is_new, 0.0, weight).astype(jnp.bfloat16))
-        new_weights.append(jnp.sum(jnp.where(is_new, weight, 0.0), axis=1, keepdims=True))
+        weights.append(
+            jnp.where(visible[j], jnp.exp(masked[j] - peak), 0.0).astype(jnp.bfloat16)
+        )
+        weight = weights[j].astype(jnp.float32)
         group_peaks = jnp.where(lane == j, peak, group_peaks)
         sums = jnp.where(lane == j, jnp.sum(weight, axis=1, keepdims=True), sums)
     group_sums = jnp.zeros((heads, LANES), jnp.float32)
@@ -366,7 +450,6 @@
         leads = jnp.where(lane == j, 1.0 - earlier, leads)
         inverse = jnp.where(total > 0.0, 1.0 / jnp.where(total > 0.0, total, 1.0), 0.0)
         piece = jnp.dot(weights[j], cache[j, 1], preferred_element_type=jnp.float32)
-        piece = piece + new_weights[j] * value_rows[j : j + 1]
         piece = jnp.where(head_mask, piece * inverse, 0.0)
         lines.append(jnp.sum(piece, axis=0, keepdims=True))
     for j in range(0, blocks, GROUP):
@@ -383,50 +466,95 @@
         stats = stats - piece.astype(jnp.float32)
     outputs = Gather(pool, (o0, o1, o2, o3, o4, o5), where, blocks)
     outputs.start()
+    news.cross()
     outputs.relay()
-
-    rows_ref[:, :columns] = key_rows.astype(jnp.bfloat16)
-    rows_ref[:, columns:] = value_rows.astype(jnp.bfloat16)
+    news.finish()
+
+    for part in range(2):
+        at = slice(part * columns, (part + 1) * columns)
+        rows_ref[:, at] = picked(fresh_pool[:, :, :, :, at]).astype(jnp.bfloat16)
+    head_rows = jnp.where(head_mask, 1.0, 0.0).astype(jnp.bfloat16)
+    product = query_pool[...].astype(jnp.float32) * fresh_pool[:, :, :, :, :columns].astype(
+        jnp.float32
+    )
+    product = product.reshape(requests, columns)
+    high = product.astype(jnp.bfloat16)
+    low = (product - high.astype(jnp.float32)).astype(jnp.bfloat16)
+    new_scores = sum(
+        lax.dot_general(
+            head_rows, piece, (((1,), (1,)), ((), ())), preferred_element_type=jnp.float32
+        )
+        for piece in (high, low)
+    )
     outputs.cross()
+
+    devices = SIDE * SIDE
+    request = lax.broadcasted_iota(jnp.int32, (requests, devices * quarter), 0).astype(jnp.float32)
+
+    def side(c):
+        fields = [[] for _ in range(4)]
+        for start in range(0, devices, 4):
+            tiles = []
+            for d in range(start, start + 4):
+                tile = pool[c, d // SIDE, d % SIDE, :, columns:].astype(jnp.float32)
+                tiles.append(tile[:8] + tile[8:16] + tile[16:24])
+            for f in range(4):
+                merged = jnp.zeros((heads, LANES), jnp.float32)
+                for k in range(4):
+                    shift = (k - f) * quarter % LANES
+                    tile = tiles[k] if shift == 0 else pltpu.roll(tiles[k], shift, 1)
+                    merged = jnp.where(lane // quarter == k, tile, merged)
+                fields[f].append(merged)
+        fields = [jnp.concatenate(f, axis=1) for f in fields]
+        used = lax.broadcasted_iota(jnp.int32, fields[3].shape, 1) % quarter < blocks
+        fields[3] = jnp.where(used, fields[3], float(requests))
+        is_long = jnp.zeros(fields[3].shape, jnp.bool_)
+        for long_id in long_ids:
+            is_long = is_long | (fields[3] == long_id)
+        short_owner = jnp.where(is_long, float(requests), fields[3])[:1]
+        member = jnp.where(request == short_owner, 1.0, 0.0).astype(jnp.bfloat16)
+        values = pool[c, :, :, :, :columns].reshape(devices * quarter, columns)
+        led = jnp.concatenate(
+            [thirds(jnp.where(fields[2] > 0.5, fields[f], 0.0)) for f in range(2)], axis=0
+        ).astype(jnp.bfloat16)
+        by_request = lax.dot_general(
+            led, member, (((1,), (1,)), ((), ())), preferred_element_type=jnp.float32
+        )
+        rows = jnp.dot(member, values, preferred_element_type=jnp.float32)
+        return fields, values, rows, by_request
+
+    near_fields, near_values, attended, by_request = side(core)
     outputs.finish()
-
-    devices = 2 * SIDE * SIDE
-    fields = [[] for _ in range(4)]
-    for start in range(0, devices, 4):
-        tiles = []
-        for d in range(start, start + 4):
-            tile = pool[
-                d // (SIDE * SIDE), d // SIDE % SIDE, d % SIDE, :, columns:
-            ].astype(jnp.float32)
-            tiles.append(tile[:8] + tile[8:16] + tile[16:24])
-        for f in range(4):
-            merged = jnp.zeros((heads, LANES), jnp.float32)
-            for k in range(4):
-                shift = (k - f) * quarter % LANES
-                tile = tiles[k] if shift == 0 else pltpu.roll(tiles[k], shift, 1)
-                merged = jnp.where(lane // quarter == k, tile, merged)
-            fields[f].append(merged)
-    peaks, sums, leads, slot_owners = [jnp.concatenate(f, axis=1) for f in fields]
-    used = lax.broadcasted_iota(jnp.int32, slot_owners.shape, 1) % quarter < blocks
-    slot_owners = jnp.where(used, slot_owners, float(requests))
+    far_fields, far_values, rest, by_request_rest = side(1 - core)
+    attended = attended + rest
+    by_request = by_request + by_request_rest
+    old_peak, old_mass = [
+        by_request[i : i + heads]
+        + by_request[i + heads : i + 2 * heads]
+        + by_request[i + 2 * heads : i + 3 * heads]
+        for i in (0, 3 * heads)
+    ]
+    request_lane = lax.broadcasted_iota(jnp.int32, (heads, requests), 1).astype(jnp.float32)
+    peaks, sums, leads, slot_owners = [
+        jnp.concatenate(pair, axis=1) for pair in zip(near_fields, far_fields)
+    ]
     high_rows, low_rows = [], []
-    is_long = jnp.zeros(slot_owners.shape, jnp.bool_)
     for long_id in long_ids:
         match = slot_owners == long_id
-        is_long = is_long | match
         peak = jnp.max(jnp.where(match, peaks, NEG_FLOOR), axis=1, keepdims=True)
         mass = jnp.where(match, sums * jnp.exp(jnp.where(match, peaks, NEG_FLOOR) - peak), 0.0)
-        weight = mass / jnp.sum(jnp.where(match, mass * leads, 0.0), axis=1, keepdims=True)
+        whole_mass = jnp.sum(jnp.where(match, mass * leads, 0.0), axis=1, keepdims=True)
+        weight = mass / whole_mass
+        old_peak = jnp.where(request_lane == long_id, peak, old_peak)
+        old_mass = jnp.where(request_lane == long_id, whole_mass, old_mass)
         high = weight.astype(jnp.bfloat16).astype(jnp.float32)
         high_rows.append(high)
         low_rows.append(weight - high)
-    request = lax.broadcasted_iota(jnp.int32, (requests, devices * quarter), 0)
-    short_owner = jnp.where(is_long, float(requests), slot_owners)[:1]
-    member = jnp.where(request.astype(jnp.float32) == short_owner, 1.0, 0.0).astype(jnp.bfloat16)
     extra = jnp.concatenate(high_rows + low_rows, axis=0).astype(jnp.bfloat16)
-    values = pool[:, :, :, :, :columns].reshape(devices * quarter, columns)
-    attended = jnp.dot(member, values, preferred_element_type=jnp.float32)
-    weighted = jnp.dot(extra, values, preferred_element_type=jnp.float32)
+    split = devices * quarter
+    weighted = jnp.dot(
+        extra[:, :split], near_values, preferred_element_type=jnp.float32
+    ) + jnp.dot(extra[:, split:], far_values, preferred_element_type=jnp.float32)
     row = lax.broadcasted_iota(jnp.int32, (requests, 1), 0).astype(jnp.float32)
     half = LONG_REQS * heads
     for l, long_id in enumerate(long_ids):
@@ -435,12 +563,28 @@
         ]
         line = jnp.sum(jnp.where(head_mask, both, 0.0), axis=0, keepdims=True)
         attended = jnp.where(row == long_id, line, attended)
+    share = 1.0 / (1.0 + old_mass * jnp.exp(old_peak - new_scores))
+    share = jnp.concatenate(
+        [share, jnp.zeros((LANES - heads, requests), jnp.float32)], axis=0
+    ).T
+    head_tall = jnp.concatenate(
+        [head_rows.astype(jnp.float32), jnp.zeros((LANES - heads, columns), jnp.float32)], axis=0
+    ).astype(jnp.bfloat16)
+    high = share.astype(jnp.bfloat16)
+    low = (share - high.astype(jnp.float32)).astype(jnp.bfloat16)
+    spread = sum(
+        jnp.dot(piece, head_tall, preferred_element_type=jnp.float32) for piece in (high, low)
+    )
+    new_values = fresh_pool[:, :, :, :, columns:].astype(jnp.float32).reshape(requests, columns)
+    attended = attended + spread * (new_values - attended)
     result = lax.dot_general(
         attended.astype(jnp.bfloat16), w_out_ref[...], (((1,), (1,)), ((), ())),
         preferred_element_type=jnp.float32,
     )
     share = requests // SIDE
-    terms[...] = result.reshape(SIDE, share, result.shape[1])
+    result = result.reshape(SIDE, share, result.shape[1])
+    exact[...] = result
+    terms[...] = result.astype(jnp.bfloat16)
     copies = [
         send(terms.at[sides[i]], arrived.at[i], sem4s.at[i], sem4r.at[i], "tp", sides[i])
         for i in range(SIDE - 1)
@@ -450,16 +594,13 @@
         for i in range(requests // LANES)
     ]
     pair = jnp.where(tp // 2 == 0, pairs[0], pairs[1])
-    total = terms[tp] + jnp.where(tp % 2 == 0, pair[:share], pair[share:])
+    total = exact[tp] + jnp.where(tp % 2 == 0, pair[:share], pair[share:])
     for copy in copies:
         copy.wait_recv()
     for i in range(SIDE - 1):
-        total = total + arrived[i]
+        total = total + arrived[i].astype(jnp.float32)
     hidden_ref[...] = total.astype(jnp.bfloat16)
-    for group in (copies0, copies1, copies2):
-        for copy in group.values():
-            copy.wait_send()
-    for gather in (queries, news, outputs):
+    for gather in (ahead, behind, queries, news, outputs):
         gather.drain()
     for copy in copies:
         copy.wait_send()
@@ -510,8 +651,6 @@
 def shards(states, norm_gain, w_qkv, w_out, cache, context_len, block_owner, block_index):
     requests, depth = states.shape
     parts, _, columns = w_qkv.shape
-    width = parts * columns
-    wide = width + LANES
     blocks = cache.shape[0]
     heads = columns // HEAD_DIM
     half_dim = HEAD_DIM // 2
@@ -525,6 +664,18 @@
     f32 = jnp.float32
     n = SIDE - 1
     share = requests // SIDE
+
+    def reduce_refs(wide):
+        return (
+            pltpu.VMEM((SIDE, SIDE, GROUP, wide), f32),
+            pltpu.VMEM((SIDE, SIDE, GROUP, wide), bf16),
+            pltpu.VMEM((SIDE, SIDE, GROUP, wide), bf16),
+            pltpu.VMEM((n, SIDE, GROUP, wide), bf16),
+            pltpu.VMEM((n, SIDE, GROUP, wide), bf16),
+            pltpu.VMEM((n, GROUP, wide), bf16),
+            pltpu.VMEM((n, GROUP, wide), bf16),
+        )
+
     gather_sems = [dma((n,)), dma((n,)), dma((SIDE, n)), dma((SIDE, n)), dma((SIDE,)), dma((SIDE,))]
     hidden, rows = pl.pallas_call(
         step_kernel,
@@ -547,26 +698,25 @@
             pltpu.VMEM((1, columns), f32),
             pltpu.VMEM(cache.shape, bf16),
             pltpu.VMEM((requests, depth), bf16),
-            pltpu.VMEM((SIDE, SIDE, GROUP, wide), f32),
-            pltpu.VMEM((SIDE, SIDE, GROUP, wide), bf16),
-            pltpu.VMEM((SIDE, SIDE, GROUP, wide), bf16),
-            pltpu.VMEM((n, SIDE, GROUP, wide), bf16),
-            pltpu.VMEM((n, SIDE, GROUP, wide), bf16),
-            pltpu.VMEM((n, GROUP, wide), bf16),
-            pltpu.VMEM((n, GROUP, wide), bf16),
+            *reduce_refs(columns + LANES),
+            *reduce_refs(2 * columns),
             pltpu.VMEM((2, SIDE, SIDE, GROUP, columns), bf16),
             pltpu.VMEM((2, SIDE, SIDE, GROUP, 2 * columns), bf16),
             pltpu.VMEM((blocks, columns), f32),
             pltpu.VMEM((blocks, heads, cache.shape[2]), f32),
             pltpu.VMEM((2, SIDE, SIDE, LANES // 4, columns + LANES), bf16),
             pltpu.VMEM((SIDE, share, depth), f32),
-            pltpu.VMEM((n, share, depth), f32),
+            pltpu.VMEM((SIDE, share, depth), bf16),
+            pltpu.VMEM((n, share, depth), bf16),
             dma((10,)),
+        ]
+        + [
             dma((SIDE,)), dma((SIDE,)),
             dma((n, SIDE)), dma((n, SIDE)),
             dma((n,)), dma((n,)),
-        ]
-        + gather_sems * 3
+        ] * 2
+        + [dma((SIDE, SIDE)), dma((SIDE, SIDE)), dma((SIDE,)), dma((SIDE,))]
+        + gather_sems * 2
         + [dma((n,)), dma((n,))],
         compiler_params=pltpu.CompilerParams(
             collective_id=0, has_side_effects=True, vmem_limit_bytes=32 << 20

time: 52.1 us -> 48.8 us (0.937)
  Pallas kernels: 51.3 us -> 47.9 us
    pallas_call x1, Pallas kernels: 47.8 us -> 44.4 us  [shards(): pl.pallas_call(step_kernel, name='step', out_shape=(jax.ShapeDtypeStruct(...]
where the time goes in v3:
time: 48.8 us; the launch traced here: 48.7 us
  Pallas kernels  47.9 us (98%)
  between operations  0.7 us (1%)
    pallas_call x1, Pallas kernels, shards(): pl.pallas_call(step_kernel, name='step', out_shape=(jax.ShapeDtypeStruct(...  44.4 us
    pallas_call x1, Pallas kernels, shards(): pl.pallas_call(store_kernel, name='store', out_shape=(jax.ShapeDtypeStruc...  3.53 us

profile of v3, /device:TPU:1, one launch (start us, length us, event | category | flops | bytes accessed | tf_op | source)
XLA Modules:
  0.0 48.7 jit_solution(14128251525649060757)
XLA Ops:
  0.6 0.0 copy-start.1
  0.6 0.0 copy-start.3
  0.7 0.0 copy-start.2
  0.7 0.0 copy-start
  0.7 44.4 %step.1 = (bf16[64,96]{1,0:T(8,128)(2,1)S(1)}, bf16[24,1536]{1,0:T(8,128)(2,1)S(1)}) custom-call(s32[256]{0:T(256)} %context_ref.1, s32[24]{0:T(128)} %owner_ref.1, s32[24]{0:T(128)} %index_ref.1, s32[2,128]{1,0:T(2,128)} %bitcast.4, bf16[96,256]{1,0:T(8,128)(2,1)} %bitcast.6, bf16[1,96]{1,0:T(2,128)(2,1)} %bitcast.7, bf16[3,96,768]{2,1,0:T(8,128)(2,1)} %w_hbm.1, ...), custom_call_target="tpu_custom_call" | custom-call | flops 1000000000 | bytes 4718592 | tf_op jit(solution)/shard_map/step/pallas_call | solution.py:680
  45.1 0.0 copy-done.1
  45.1 0.0 copy-done.3
  45.1 0.0 copy-done.2
  45.1 0.0 copy-done
  45.1 3.5 %store.1 = (bf16[64,96]{1,0:T(8,128)(2,1)}, bf16[24,2,64,768]{3,2,1,0:T(8,128)(2,1)}) custom-call(s32[256]{0:T(256)S(1)} %copy-done.1, s32[24]{0:T(128)S(1)} %copy-done.2, s32[24]{0:T(128)S(1)} %copy-done.3, bf16[64,96]{1,0:T(8,128)(2,1)S(1)} %get-tuple-element.4.hidden_in_ref, bf16[24,1536]{1,0:T(8,128)(2,1)S(1)} %get-tuple-element.5.rows_ref, ...), custom_call_target="tpu_custom_call" | custom-call | tf_op jit(solution)/shard_map/store/pallas_call | solution.py:736
Async XLA Ops:
  0.6 44.5 %copy-start.1 = (s32[256]{0:T(256)S(1)}, s32[256]{0:T(256)}, u32[]{:S(2)}) copy-start(s32[256]{0:T(256)} %context_ref.1) | copy-start | bytes 3076
  0.6 44.5 %copy-start.3 = (s32[24]{0:T(128)S(1)}, s32[24]{0:T(128)}, u32[]{:S(2)}) copy-start(s32[24]{0:T(128)} %index_ref.1) | copy-start | bytes 292
  0.7 44.5 %copy-start.2 = (s32[24]{0:T(128)S(1)}, s32[24]{0:T(128)}, u32[]{:S(2)}) copy-start(s32[24]{0:T(128)} %owner_ref.1) | copy-start | bytes 292
  0.7 44.5 %copy-start = (bf16[24,2,64,768]{3,2,1,0:T(8,128)(2,1)S(1)}, bf16[24,2,64,768]{3,2,1,0:T(8,128)(2,1)}, u32[]{:S(2)}) copy-start(bf16[24,2,64,768]{3,2,1,0:T(8,128)(2,1)} %cache_ref.1) | copy-start | bytes 14155780

commit v4 on v3

--- a/solution.py
+++ b/solution.py
@@ -280,7 +280,7 @@
     core, first, second, partner, primary, secondary, peers = where
     tp = lax.axis_index("tp")
     sides = [(tp + i) % SIDE for i in range(1, SIDE)]
-    greet("seq", [partner] + list(peers.values()))
+    greet("seq", [partner] + primary + secondary)
     greet("tp", sides)
     loads = {}
     for i, (name, source, target) in enumerate(
@@ -324,7 +324,7 @@
     ahead.snd0[:, :, :, columns:] = halves(
         jnp.where(core == 0, squares[1], squares[0])
     ).reshape(shape + (LANES,))
-    pl.semaphore_wait(pltpu.get_barrier_semaphore(), 19)
+    pl.semaphore_wait(pltpu.get_barrier_semaphore(), 10)
     ahead.swap()
     project(ahead.own, core, 0, 0)
     ahead.own[:, :, :, columns:] = jnp.where(core == 0, squares[0], squares[1]).reshape(
@@ -387,7 +387,6 @@
         long_ids.append(top)
         candidates = jnp.where(candidates == top, -1.0, candidates)
     loads["cache"].wait()
-    behind.middle()
     term, total = ahead.end()
 
     inverse = lax.rsqrt(total / (HEAD_DIM * 32) + EPSILON)[:, :1]
@@ -395,6 +394,7 @@
     query_pool[core, first, second] = query.astype(jnp.bfloat16)
     queries = Direct(query_pool, (q0, q1, q2, q3), where)
     queries.start()
+    behind.middle()
     term, _ = behind.end()
     key = rotated(term[:, :columns] * inverse, cosine, sine, is_front)
     fresh_pool[core, first, second, :, :columns] = key.astype(jnp.bfloat16)

time: 48.8 us -> 50.1 us (1.027)
  Pallas kernels: 47.9 us -> 49.3 us
    pallas_call x1, Pallas kernels: 44.4 us -> 45.7 us  [shards(): pl.pallas_call(step_kernel, name='step', out_shape=(jax.ShapeDtypeStruct(...]
where the time goes in v4:
time: 50.1 us; the launch traced here: 50 us
  Pallas kernels  49.3 us (98%)
  between operations  0.7 us (1%)
    pallas_call x1, Pallas kernels, shards(): pl.pallas_call(step_kernel, name='step', out_shape=(jax.ShapeDtypeStruct(...  45.7 us
    pallas_call x1, Pallas kernels, shards(): pl.pallas_call(store_kernel, name='store', out_shape=(jax.ShapeDtypeStruc...  3.54 us

profile of v4, /device:TPU:1, one launch (start us, length us, event | category | flops | bytes accessed | tf_op | source)
XLA Modules:
  0.0 50.0 jit_solution(15995882939498986999)
XLA Ops:
  0.6 0.0 copy-start.1
  0.6 0.0 copy-start.3
  0.7 0.0 copy-start.2
  0.7 0.0 copy-start
  0.7 45.7 %step.1 = (bf16[64,96]{1,0:T(8,128)(2,1)S(1)}, bf16[24,1536]{1,0:T(8,128)(2,1)S(1)}) custom-call(s32[256]{0:T(256)} %context_ref.1, s32[24]{0:T(128)} %owner_ref.1, s32[24]{0:T(128)} %index_ref.1, s32[2,128]{1,0:T(2,128)} %bitcast.4, bf16[96,256]{1,0:T(8,128)(2,1)} %bitcast.6, bf16[1,96]{1,0:T(2,128)(2,1)} %bitcast.7, bf16[3,96,768]{2,1,0:T(8,128)(2,1)} %w_hbm.1, ...), custom_call_target="tpu_custom_call" | custom-call | flops 1000000000 | bytes 4718592 | tf_op jit(solution)/shard_map/step/pallas_call | solution.py:680
  46.4 0.0 copy-done.1
  46.4 0.0 copy-done.3
  46.4 0.0 copy-done.2
  46.4 0.0 copy-done
  46.4 3.5 %store.1 = (bf16[64,96]{1,0:T(8,128)(2,1)}, bf16[24,2,64,768]{3,2,1,0:T(8,128)(2,1)}) custom-call(s32[256]{0:T(256)S(1)} %copy-done.1, s32[24]{0:T(128)S(1)} %copy-done.2, s32[24]{0:T(128)S(1)} %copy-done.3, bf16[64,96]{1,0:T(8,128)(2,1)S(1)} %get-tuple-element.4.hidden_in_ref, bf16[24,1536]{1,0:T(8,128)(2,1)S(1)} %get-tuple-element.5.rows_ref, ...), custom_call_target="tpu_custom_call" | custom-call | tf_op jit(solution)/shard_map/store/pallas_call | solution.py:736
Async XLA Ops:
  0.6 45.8 %copy-start.1 = (s32[256]{0:T(256)S(1)}, s32[256]{0:T(256)}, u32[]{:S(2)}) copy-start(s32[256]{0:T(256)} %context_ref.1) | copy-start | bytes 3076
  0.6 45.8 %copy-start.3 = (s32[24]{0:T(128)S(1)}, s32[24]{0:T(128)}, u32[]{:S(2)}) copy-start(s32[24]{0:T(128)} %index_ref.1) | copy-start | bytes 292
  0.7 45.8 %copy-start.2 = (s32[24]{0:T(128)S(1)}, s32[24]{0:T(128)}, u32[]{:S(2)}) copy-start(s32[24]{0:T(128)} %owner_ref.1) | copy-start | bytes 292
  0.7 45.8 %copy-start = (bf16[24,2,64,768]{3,2,1,0:T(8,128)(2,1)S(1)}, bf16[24,2,64,768]{3,2,1,0:T(8,128)(2,1)}, u32[]{:S(2)}) copy-start(bf16[24,2,64,768]{3,2,1,0:T(8,128)(2,1)} %cache_ref.1) | copy-start | bytes 14155780

commit v5 on v4

--- a/solution.py
+++ b/solution.py
@@ -88,81 +88,6 @@
     return values * cosine + other * sine
 
 
-class Reduce:
-    def __init__(self, refs, sems, where, squares):
-        self.own, self.snd0, self.rcv0, self.snd1, self.rcv1, self.snd2, self.rcv2 = refs
-        self.sems = sems
-        self.first, self.second, self.partner, self.primary, self.secondary = where[1:6]
-        self.squares = squares
-        self.width = self.own.shape[-1] - (LANES if squares else 0)
-        self.copies = []
-
-    def put(self, ref, index, body, total):
-        ref[index + (slice(None), slice(0, self.width))] = body.astype(jnp.bfloat16)
-        if self.squares:
-            ref[index + (slice(None), slice(self.width, None))] = halves(total)
-
-    def add(self, term, ref, index):
-        body, total = term
-        body = body + ref[index + (slice(None), slice(0, self.width))].astype(jnp.float32)
-        if self.squares:
-            total = total + whole(ref[index + (slice(None), slice(self.width, None))])
-        return body, total
-
-    def local(self, a, b):
-        total = self.own[a, b, :, self.width :] if self.squares else None
-        return self.add((self.own[a, b, :, : self.width], total), self.rcv0, (a, b))
-
-    def send(self, src, dst, stage, index, to):
-        copy = send(
-            src, dst, self.sems[2 * stage].at[index], self.sems[2 * stage + 1].at[index], "seq", to
-        )
-        self.copies.append(copy)
-        return copy
-
-    def swap(self):
-        self.swapped = {}
-        for i in ORDER + (0,):
-            b = (self.first + i) % SIDE
-            self.swapped[i] = self.send(self.snd0.at[:, b], self.rcv0.at[:, b], 0, i, self.partner)
-
-    def begin(self):
-        self.across = {}
-        for j in ORDER + (0,):
-            self.swapped[j].wait_recv()
-            b = (self.second + j) % SIDE
-            for i in ORDER:
-                self.put(self.snd1, (i - 1, j), *self.local((self.first + i) % SIDE, b))
-                self.across[i, j] = self.send(
-                    self.snd1.at[i - 1, j], self.rcv1.at[i - 1, j], 1, (i - 1, j),
-                    self.primary[i - 1],
-                )
-
-    def middle(self):
-        self.along = {}
-        for j in ORDER + (0,):
-            term = self.local(self.first, (self.second + j) % SIDE)
-            for i in ORDER:
-                self.across[i, j].wait_recv()
-                term = self.add(term, self.rcv1, (i - 1, j))
-            if j:
-                self.put(self.snd2, (j - 1,), *term)
-                self.along[j] = self.send(
-                    self.snd2.at[j - 1], self.rcv2.at[j - 1], 2, j - 1, self.secondary[j - 1]
-                )
-        self.term = term
-
-    def end(self):
-        for j in (1, 3, 2):
-            self.along[j].wait_recv()
-            self.term = self.add(self.term, self.rcv2, (j - 1,))
-        return self.term
-
-    def drain(self):
-        for copy in self.copies:
-            copy.wait_send()
-
-
 class Gather:
     def __init__(self, ref, sems, where, part=None):
         self.ref, self.part = ref, part
@@ -271,10 +196,10 @@
     frequency_hbm, cache_hbm,
     hidden_ref, rows_ref,
     context_ref, owner_ref, index_ref, lens_ref, states_ref, gain_ref, w_ref, w_out_ref,
-    frequency_ref, cache, scaled, a0, a1, a2, a3, a4, a5, a6, b0, b1, b2, b3, b4, b5, b6, query_pool, fresh_pool, query_rows,
-    scores, pool, exact, terms, arrived,
-    sem_in, c0, c1, c2, c3, c4, c5, d0, d1, d2, d3, d4, d5,
-    q0, q1, q2, q3, k0, k1, k2, k3, k4, k5, o0, o1, o2, o3, o4, o5, sem4s, sem4r,
+    frequency_ref, cache, scaled, own, snd0, rcv0, snd1, rcv1, snd2, rcv2, query_pool, fresh_pool, query_rows,
+    scores, table, shares, old, pool, exact, terms, arrived,
+    sem_in, sem0s, sem0r, sem1s, sem1r, sem2s, sem2r,
+    q0, q1, q2, q3, t0, t1, t2, t3, k0, k1, k2, k3, k4, k5, o0, o1, o2, o3, o4, o5, sem4s, sem4r,
 ):
     where = place()
     core, first, second, partner, primary, secondary, peers = where
@@ -296,6 +221,7 @@
         loads[name].start()
 
     parts, _, columns = w_ref.shape
+    width = parts * columns
     blocks, _, tokens, _ = cache.shape
     heads = columns // HEAD_DIM
     requests = context_ref.shape[0]
@@ -310,33 +236,42 @@
     squares = [squares[:half_rows], squares[half_rows:]]
     shape = (SIDE, SIDE, GROUP)
     loads["w"].wait()
-    ahead = Reduce((a0, a1, a2, a3, a4, a5, a6), (c0, c1, c2, c3, c4, c5), where, True)
-    behind = Reduce((b0, b1, b2, b3, b4, b5, b6), (d0, d1, d2, d3, d4, d5), where, False)
-
-    def project(ref, side, part, at):
-        rows = scaled[pl.ds(pl.multiple_of(side * half_rows, half_rows), half_rows), :]
+    rows = scaled[pl.ds(pl.multiple_of((1 - core) * half_rows, half_rows), half_rows), :]
+    for part in range(parts):
         term = jnp.dot(rows, w_ref[part], preferred_element_type=jnp.float32)
-        ref[:, :, :, at * columns : (at + 1) * columns] = term.reshape(
+        snd0[:, :, :, part * columns : (part + 1) * columns] = term.reshape(
             shape + (columns,)
-        ).astype(ref.dtype)
-
-    project(ahead.snd0, 1 - core, 0, 0)
-    ahead.snd0[:, :, :, columns:] = halves(
-        jnp.where(core == 0, squares[1], squares[0])
-    ).reshape(shape + (LANES,))
+        ).astype(jnp.bfloat16)
+    snd0[:, :, :, width:] = halves(jnp.where(core == 0, squares[1], squares[0])).reshape(
+        shape + (LANES,)
+    )
     pl.semaphore_wait(pltpu.get_barrier_semaphore(), 10)
-    ahead.swap()
-    project(ahead.own, core, 0, 0)
-    ahead.own[:, :, :, columns:] = jnp.where(core == 0, squares[0], squares[1]).reshape(
-        shape + (LANES,)
-    )
-    project(behind.snd0, 1 - core, 1, 0)
-    project(behind.snd0, 1 - core, 2, 1)
-    behind.swap()
-    ahead.begin()
-    project(behind.own, core, 1, 0)
-    project(behind.own, core, 2, 1)
-    behind.begin()
+    copies0 = {}
+    for i in ORDER + (0,):
+        b = (first + i) % SIDE
+        copies0[i] = send(
+            snd0.at[:, b], rcv0.at[:, b], sem0s.at[i], sem0r.at[i], "seq", partner
+        )
+    rows = scaled[pl.ds(pl.multiple_of(core * half_rows, half_rows), half_rows), :]
+    for part in range(parts):
+        term = jnp.dot(rows, w_ref[part], preferred_element_type=jnp.float32)
+        own[:, :, :, part * columns : (part + 1) * columns] = term.reshape(shape + (columns,))
+    own[:, :, :, width:] = jnp.where(core == 0, squares[0], squares[1]).reshape(shape + (LANES,))
+
+    copies1 = {}
+    for j in ORDER + (0,):
+        copies0[j].wait_recv()
+        b = (second + j) % SIDE
+        for i in ORDER:
+            a = (first + i) % SIDE
+            snd1[i - 1, j, :, :width] = (
+                own[a, b, :, :width] + rcv0[a, b, :, :width].astype(jnp.float32)
+            ).astype(jnp.bfloat16)
+            snd1[i - 1, j, :, width:] = halves(own[a, b, :, width:] + whole(rcv0[a, b, :, width:]))
+            copies1[i, j] = send(
+                snd1.at[i - 1, j], rcv1.at[i - 1, j], sem1s.at[i - 1, j], sem1r.at[i - 1, j],
+                "seq", primary[i - 1],
+            )
 
     for name in ("context", "owner", "index", "lens", "frequency", "w_out"):
         loads[name].wait()
@@ -350,7 +285,23 @@
     is_front = lax.broadcasted_iota(jnp.int32, (GROUP, columns), 1) % HEAD_DIM < HEAD_DIM // 2
     sine = jnp.sin(angle)
     sine = jnp.where(is_front, -sine, sine)
-    ahead.middle()
+
+    copies2 = {}
+    for j in ORDER + (0,):
+        b = (second + j) % SIDE
+        term = own[first, b, :, :width] + rcv0[first, b, :, :width].astype(jnp.float32)
+        total = own[first, b, :, width:] + whole(rcv0[first, b, :, width:])
+        for i in ORDER:
+            copies1[i, j].wait_recv()
+            term = term + rcv1[i - 1, j, :, :width].astype(jnp.float32)
+            total = total + whole(rcv1[i - 1, j, :, width:])
+        if j:
+            snd2[j - 1, :, :width] = term.astype(jnp.bfloat16)
+            snd2[j - 1, :, width:] = halves(total)
+            copies2[j] = send(
+                snd2.at[j - 1], rcv2.at[j - 1], sem2s.at[j - 1], sem2r.at[j - 1],
+                "seq", secondary[j - 1],
+            )
     slot = lax.broadcasted_iota(jnp.int32, (blocks, requests), 0)
     wanted = jnp.zeros((blocks, requests), jnp.int32)
     lane = lax.broadcasted_iota(jnp.int32, (heads, LANES), 1)
@@ -387,18 +338,19 @@
         long_ids.append(top)
         candidates = jnp.where(candidates == top, -1.0, candidates)
     loads["cache"].wait()
-    term, total = ahead.end()
+    for j in (1, 3, 2):
+        copies2[j].wait_recv()
+        term = term + rcv2[j - 1, :, :width].astype(jnp.float32)
+        total = total + whole(rcv2[j - 1, :, width:])
 
     inverse = lax.rsqrt(total / (HEAD_DIM * 32) + EPSILON)[:, :1]
-    query = rotated(term * inverse, cosine, sine, is_front) * HEAD_DIM ** (-0.5)
+    query = rotated(term[:, :columns] * inverse, cosine, sine, is_front) * HEAD_DIM ** (-0.5)
     query_pool[core, first, second] = query.astype(jnp.bfloat16)
     queries = Direct(query_pool, (q0, q1, q2, q3), where)
     queries.start()
-    behind.middle()
-    term, _ = behind.end()
-    key = rotated(term[:, :columns] * inverse, cosine, sine, is_front)
+    key = rotated(term[:, columns : 2 * columns] * inverse, cosine, sine, is_front)
     fresh_pool[core, first, second, :, :columns] = key.astype(jnp.bfloat16)
-    fresh_pool[core, first, second, :, columns:] = (term[:, columns:] * inverse).astype(
+    fresh_pool[core, first, second, :, columns:] = (term[:, 2 * columns :] * inverse).astype(
         jnp.bfloat16
     )
     news = Gather(fresh_pool, (k0, k1, k2, k3, k4, k5), where)
@@ -441,38 +393,37 @@
         sums = jnp.where(lane == j, jnp.sum(weight, axis=1, keepdims=True), sums)
     group_sums = jnp.zeros((heads, LANES), jnp.float32)
     leads = jnp.zeros((heads, LANES), jnp.float32)
-    lines = []
+    inverses = []
     for j in range(blocks):
         same = owner_lanes == owners[j]
         total = jnp.sum(jnp.where(same, sums, 0.0), axis=1, keepdims=True)
         group_sums = jnp.where(lane == j, total, group_sums)
         earlier = jnp.max(jnp.where(same & (lane < j), 1.0, 0.0), axis=1, keepdims=True)
         leads = jnp.where(lane == j, 1.0 - earlier, leads)
-        inverse = jnp.where(total > 0.0, 1.0 / jnp.where(total > 0.0, total, 1.0), 0.0)
-        piece = jnp.dot(weights[j], cache[j, 1], preferred_element_type=jnp.float32)
-        piece = jnp.where(head_mask, piece * inverse, 0.0)
-        lines.append(jnp.sum(piece, axis=0, keepdims=True))
-    for j in range(0, blocks, GROUP):
-        pool[core, first, second, j : j + GROUP, :columns] = jnp.concatenate(
-            lines[j : j + GROUP], axis=0
-        ).astype(jnp.bfloat16)
+        inverses.append(jnp.where(total > 0.0, 1.0 / jnp.where(total > 0.0, total, 1.0), 0.0))
     quarter = LANES // 4
     stats = group_peaks
     for f, field in enumerate((group_sums, leads, owner_lanes.astype(jnp.float32))):
         stats = jnp.where(lane // quarter == f + 1, pltpu.roll(field, (f + 1) * quarter, 1), stats)
+    table[core, first, second] = stats
+    tables = Direct(table, (t0, t1, t2, t3), where)
+    tables.start()
+    lines = []
+    for j in range(blocks):
+        piece = jnp.dot(weights[j], cache[j, 1], preferred_element_type=jnp.float32)
+        piece = jnp.where(head_mask, piece * inverses[j], 0.0)
+        lines.append(jnp.sum(piece, axis=0, keepdims=True))
     for j in range(0, blocks, GROUP):
-        piece = stats.astype(jnp.bfloat16)
-        pool[core, first, second, j : j + GROUP, columns:] = piece
-        stats = stats - piece.astype(jnp.float32)
+        pool[core, first, second, j : j + GROUP, :] = jnp.concatenate(
+            lines[j : j + GROUP], axis=0
+        ).astype(jnp.bfloat16)
     outputs = Gather(pool, (o0, o1, o2, o3, o4, o5), where, blocks)
     outputs.start()
     news.cross()
     outputs.relay()
+    tables.cross((0, 1, 3, 2))
     news.finish()
 
-    for part in range(2):
-        at = slice(part * columns, (part + 1) * columns)
-        rows_ref[:, at] = picked(fresh_pool[:, :, :, :, at]).astype(jnp.bfloat16)
     head_rows = jnp.where(head_mask, 1.0, 0.0).astype(jnp.bfloat16)
     product = query_pool[...].astype(jnp.float32) * fresh_pool[:, :, :, :, :columns].astype(
         jnp.float32
@@ -486,18 +437,16 @@
         )
         for piece in (high, low)
     )
-    outputs.cross()
+    tables.finish()
 
     devices = SIDE * SIDE
-    request = lax.broadcasted_iota(jnp.int32, (requests, devices * quarter), 0).astype(jnp.float32)
+    split = devices * quarter
+    request = lax.broadcasted_iota(jnp.int32, (requests, split), 0).astype(jnp.float32)
 
     def side(c):
         fields = [[] for _ in range(4)]
         for start in range(0, devices, 4):
-            tiles = []
-            for d in range(start, start + 4):
-                tile = pool[c, d // SIDE, d % SIDE, :, columns:].astype(jnp.float32)
-                tiles.append(tile[:8] + tile[8:16] + tile[16:24])
+            tiles = [table[c, d // SIDE, d % SIDE] for d in range(start, start + 4)]
             for f in range(4):
                 merged = jnp.zeros((heads, LANES), jnp.float32)
                 for k in range(4):
@@ -513,20 +462,16 @@
             is_long = is_long | (fields[3] == long_id)
         short_owner = jnp.where(is_long, float(requests), fields[3])[:1]
         member = jnp.where(request == short_owner, 1.0, 0.0).astype(jnp.bfloat16)
-        values = pool[c, :, :, :, :columns].reshape(devices * quarter, columns)
         led = jnp.concatenate(
             [thirds(jnp.where(fields[2] > 0.5, fields[f], 0.0)) for f in range(2)], axis=0
         ).astype(jnp.bfloat16)
         by_request = lax.dot_general(
             led, member, (((1,), (1,)), ((), ())), preferred_element_type=jnp.float32
         )
-        rows = jnp.dot(member, values, preferred_element_type=jnp.float32)
-        return fields, values, rows, by_request
-
-    near_fields, near_values, attended, by_request = side(core)
-    outputs.finish()
-    far_fields, far_values, rest, by_request_rest = side(1 - core)
-    attended = attended + rest
+        return fields, member, by_request
+
+    near_fields, near_member, by_request = side(core)
+    far_fields, far_member, by_request_rest = side(1 - core)
     by_request = by_request + by_request_rest
     old_peak, old_mass = [
         by_request[i : i + heads]
@@ -551,18 +496,6 @@
         high_rows.append(high)
         low_rows.append(weight - high)
     extra = jnp.concatenate(high_rows + low_rows, axis=0).astype(jnp.bfloat16)
-    split = devices * quarter
-    weighted = jnp.dot(
-        extra[:, :split], near_values, preferred_element_type=jnp.float32
-    ) + jnp.dot(extra[:, split:], far_values, preferred_element_type=jnp.float32)
-    row = lax.broadcasted_iota(jnp.int32, (requests, 1), 0).astype(jnp.float32)
-    half = LONG_REQS * heads
-    for l, long_id in enumerate(long_ids):
-        both = weighted[l * heads : (l + 1) * heads] + weighted[
-            half + l * heads : half + (l + 1) * heads
-        ]
-        line = jnp.sum(jnp.where(head_mask, both, 0.0), axis=0, keepdims=True)
-        attended = jnp.where(row == long_id, line, attended)
     share = 1.0 / (1.0 + old_mass * jnp.exp(old_peak - new_scores))
     share = jnp.concatenate(
         [share, jnp.zeros((LANES - heads, requests), jnp.float32)], axis=0
@@ -572,11 +505,28 @@
     ).astype(jnp.bfloat16)
     high = share.astype(jnp.bfloat16)
     low = (share - high.astype(jnp.float32)).astype(jnp.bfloat16)
-    spread = sum(
+    shares[...] = sum(
         jnp.dot(piece, head_tall, preferred_element_type=jnp.float32) for piece in (high, low)
     )
+    row = lax.broadcasted_iota(jnp.int32, (requests, 1), 0).astype(jnp.float32)
+    half = LONG_REQS * heads
+
+    outputs.cross()
+    values = pool[core].reshape(split, columns)
+    old[...] = jnp.dot(near_member, values, preferred_element_type=jnp.float32)
+    weighted = jnp.dot(extra[:, :split], values, preferred_element_type=jnp.float32)
+    outputs.finish()
+    values = pool[1 - core].reshape(split, columns)
+    attended = old[...] + jnp.dot(far_member, values, preferred_element_type=jnp.float32)
+    weighted = weighted + jnp.dot(extra[:, split:], values, preferred_element_type=jnp.float32)
+    for l, long_id in enumerate(long_ids):
+        both = weighted[l * heads : (l + 1) * heads] + weighted[
+            half + l * heads : half + (l + 1) * heads
+        ]
+        line = jnp.sum(jnp.where(head_mask, both, 0.0), axis=0, keepdims=True)
+        attended = jnp.where(row == long_id, line, attended)
     new_values = fresh_pool[:, :, :, :, columns:].astype(jnp.float32).reshape(requests, columns)
-    attended = attended + spread * (new_values - attended)
+    attended = attended + shares[...] * (new_values - attended)
     result = lax.dot_general(
         attended.astype(jnp.bfloat16), w_out_ref[...], (((1,), (1,)), ((), ())),
         preferred_element_type=jnp.float32,
@@ -589,6 +539,9 @@
         send(terms.at[sides[i]], arrived.at[i], sem4s.at[i], sem4r.at[i], "tp", sides[i])
         for i in range(SIDE - 1)
     ]
+    for part in range(2):
+        at = slice(part * columns, (part + 1) * columns)
+        rows_ref[:, at] = picked(fresh_pool[:, :, :, :, at]).astype(jnp.bfloat16)
     pairs = [
         states_ref[:, i * LANES : (i + 1) * LANES].astype(jnp.float32).T
         for i in range(requests // LANES)
@@ -600,7 +553,10 @@
     for i in range(SIDE - 1):
         total = total + arrived[i].astype(jnp.float32)
     hidden_ref[...] = total.astype(jnp.bfloat16)
-    for gather in (ahead, behind, queries, news, outputs):
+    for group in (copies0, copies1, copies2):
+        for copy in group.values():
+            copy.wait_send()
+    for gather in (queries, news, tables, outputs):
         gather.drain()
     for copy in copies:
         copy.wait_send()
@@ -651,6 +607,8 @@
 def shards(states, norm_gain, w_qkv, w_out, cache, context_len, block_owner, block_index):
     requests, depth = states.shape
     parts, _, columns = w_qkv.shape
+    width = parts * columns
+    wide = width + LANES
     blocks = cache.shape[0]
     heads = columns // HEAD_DIM
     half_dim = HEAD_DIM // 2
@@ -664,18 +622,6 @@
     f32 = jnp.float32
     n = SIDE - 1
     share = requests // SIDE
-
-    def reduce_refs(wide):
-        return (
-            pltpu.VMEM((SIDE, SIDE, GROUP, wide), f32),
-            pltpu.VMEM((SIDE, SIDE, GROUP, wide), bf16),
-            pltpu.VMEM((SIDE, SIDE, GROUP, wide), bf16),
-            pltpu.VMEM((n, SIDE, GROUP, wide), bf16),
-            pltpu.VMEM((n, SIDE, GROUP, wide), bf16),
-            pltpu.VMEM((n, GROUP, wide), bf16),
-            pltpu.VMEM((n, GROUP, wide), bf16),
-        )
-
     gather_sems = [dma((n,)), dma((n,)), dma((SIDE, n)), dma((SIDE, n)), dma((SIDE,)), dma((SIDE,))]
     hidden, rows = pl.pallas_call(
         step_kernel,
@@ -698,24 +644,30 @@
             pltpu.VMEM((1, columns), f32),
             pltpu.VMEM(cache.shape, bf16),
             pltpu.VMEM((requests, depth), bf16),
-            *reduce_refs(columns + LANES),
-            *reduce_refs(2 * columns),
+            pltpu.VMEM((SIDE, SIDE, GROUP, wide), f32),
+            pltpu.VMEM((SIDE, SIDE, GROUP, wide), bf16),
+            pltpu.VMEM((SIDE, SIDE, GROUP, wide), bf16),
+            pltpu.VMEM((n, SIDE, GROUP, wide), bf16),
+            pltpu.VMEM((n, SIDE, GROUP, wide), bf16),
+            pltpu.VMEM((n, GROUP, wide), bf16),
+            pltpu.VMEM((n, GROUP, wide), bf16),
             pltpu.VMEM((2, SIDE, SIDE, GROUP, columns), bf16),
             pltpu.VMEM((2, SIDE, SIDE, GROUP, 2 * columns), bf16),
             pltpu.VMEM((blocks, columns), f32),
             pltpu.VMEM((blocks, heads, cache.shape[2]), f32),
-            pltpu.VMEM((2, SIDE, SIDE, LANES // 4, columns + LANES), bf16),
+            pltpu.VMEM((2, SIDE, SIDE, heads, LANES), f32),
+            pltpu.VMEM((requests, columns), f32),
+            pltpu.VMEM((requests, columns), f32),
+            pltpu.VMEM((2, SIDE, SIDE, LANES // 4, columns), bf16),
             pltpu.VMEM((SIDE, share, depth), f32),
             pltpu.VMEM((SIDE, share, depth), bf16),
             pltpu.VMEM((n, share, depth), bf16),
             dma((10,)),
-        ]
-        + [
             dma((SIDE,)), dma((SIDE,)),
             dma((n, SIDE)), dma((n, SIDE)),
             dma((n,)), dma((n,)),
-        ] * 2
-        + [dma((SIDE, SIDE)), dma((SIDE, SIDE)), dma((SIDE,)), dma((SIDE,))]
+        ]
+        + [dma((SIDE, SIDE)), dma((SIDE, SIDE)), dma((SIDE,)), dma((SIDE,))] * 2
         + gather_sems * 2
         + [dma((n,)), dma((n,))],
         compiler_params=pltpu.CompilerParams(

time: 50.1 us -> 47.2 us (0.942)
  Pallas kernels: 49.3 us -> 46.4 us
    pallas_call x1, Pallas kernels: 45.7 us -> 42.9 us  [shards(): pl.pallas_call(step_kernel, name='step', out_shape=(jax.ShapeDtypeStruct(...]
where the time goes in v5:
time: 47.2 us; the launch traced here: 47.1 us
  Pallas kernels  46.4 us (98%)
  between operations  0.7 us (1%)
    pallas_call x1, Pallas kernels, shards(): pl.pallas_call(step_kernel, name='step', out_shape=(jax.ShapeDtypeStruct(...  42.9 us
    pallas_call x1, Pallas kernels, shards(): pl.pallas_call(store_kernel, name='store', out_shape=(jax.ShapeDtypeStruc...  3.54 us

profile of v5, /device:TPU:1, one launch (start us, length us, event | category | flops | bytes accessed | tf_op | source)
XLA Modules:
  0.0 47.1 jit_solution(17721154107088145864)
XLA Ops:
  0.6 0.0 copy-start.1
  0.6 0.0 copy-start.3
  0.7 0.0 copy-start.2
  0.7 0.0 copy-start
  0.7 42.9 %step.1 = (bf16[64,96]{1,0:T(8,128)(2,1)S(1)}, bf16[24,1536]{1,0:T(8,128)(2,1)S(1)}) custom-call(s32[256]{0:T(256)} %context_ref.1, s32[24]{0:T(128)} %owner_ref.1, s32[24]{0:T(128)} %index_ref.1, s32[2,128]{1,0:T(2,128)} %bitcast.4, bf16[96,256]{1,0:T(8,128)(2,1)} %bitcast.6, bf16[1,96]{1,0:T(2,128)(2,1)} %bitcast.7, bf16[3,96,768]{2,1,0:T(8,128)(2,1)} %w_hbm.1, ...), custom_call_target="tpu_custom_call" | custom-call | flops 1000000000 | bytes 4718592 | tf_op jit(solution)/shard_map/step/pallas_call | solution.py:626
  43.5 0.0 copy-done.1
  43.5 0.0 copy-done.3
  43.6 0.0 copy-done.2
  43.6 0.0 copy-done
  43.6 3.5 %store.1 = (bf16[64,96]{1,0:T(8,128)(2,1)}, bf16[24,2,64,768]{3,2,1,0:T(8,128)(2,1)}) custom-call(s32[256]{0:T(256)S(1)} %copy-done.1, s32[24]{0:T(128)S(1)} %copy-done.2, s32[24]{0:T(128)S(1)} %copy-done.3, bf16[64,96]{1,0:T(8,128)(2,1)S(1)} %get-tuple-element.4.hidden_in_ref, bf16[24,1536]{1,0:T(8,128)(2,1)S(1)} %get-tuple-element.5.rows_ref, ...), custom_call_target="tpu_custom_call" | custom-call | tf_op jit(solution)/shard_map/store/pallas_call | solution.py:688
Async XLA Ops:
  0.6 42.9 %copy-start.1 = (s32[256]{0:T(256)S(1)}, s32[256]{0:T(256)}, u32[]{:S(2)}) copy-start(s32[256]{0:T(256)} %context_ref.1) | copy-start | bytes 3076
  0.6 42.9 %copy-start.3 = (s32[24]{0:T(128)S(1)}, s32[24]{0:T(128)}, u32[]{:S(2)}) copy-start(s32[24]{0:T(128)} %index_ref.1) | copy-start | bytes 292
  0.7 42.9 %copy-start.2 = (s32[24]{0:T(128)S(1)}, s32[24]{0:T(128)}, u32[]{:S(2)}) copy-start(s32[24]{0:T(128)} %owner_ref.1) | copy-start | bytes 292
  0.7 42.9 %copy-start = (bf16[24,2,64,768]{3,2,1,0:T(8,128)(2,1)S(1)}, bf16[24,2,64,768]{3,2,1,0:T(8,128)(2,1)}, u32[]{:S(2)}) copy-start(bf16[24,2,64,768]{3,2,1,0:T(8,128)(2,1)} %cache_ref.1) | copy-start | bytes 14155780

commit v6 on v5

--- a/solution.py
+++ b/solution.py
@@ -422,21 +422,7 @@
     news.cross()
     outputs.relay()
     tables.cross((0, 1, 3, 2))
-    news.finish()
-
-    head_rows = jnp.where(head_mask, 1.0, 0.0).astype(jnp.bfloat16)
-    product = query_pool[...].astype(jnp.float32) * fresh_pool[:, :, :, :, :columns].astype(
-        jnp.float32
-    )
-    product = product.reshape(requests, columns)
-    high = product.astype(jnp.bfloat16)
-    low = (product - high.astype(jnp.float32)).astype(jnp.bfloat16)
-    new_scores = sum(
-        lax.dot_general(
-            head_rows, piece, (((1,), (1,)), ((), ())), preferred_element_type=jnp.float32
-        )
-        for piece in (high, low)
-    )
+
     tables.finish()
 
     devices = SIDE * SIDE
@@ -496,6 +482,21 @@
         high_rows.append(high)
         low_rows.append(weight - high)
     extra = jnp.concatenate(high_rows + low_rows, axis=0).astype(jnp.bfloat16)
+    outputs.cross()
+    news.finish()
+    head_rows = jnp.where(head_mask, 1.0, 0.0).astype(jnp.bfloat16)
+    product = query_pool[...].astype(jnp.float32) * fresh_pool[:, :, :, :, :columns].astype(
+        jnp.float32
+    )
+    product = product.reshape(requests, columns)
+    high = product.astype(jnp.bfloat16)
+    low = (product - high.astype(jnp.float32)).astype(jnp.bfloat16)
+    new_scores = sum(
+        lax.dot_general(
+            head_rows, piece, (((1,), (1,)), ((), ())), preferred_element_type=jnp.float32
+        )
+        for piece in (high, low)
+    )
     share = 1.0 / (1.0 + old_mass * jnp.exp(old_peak - new_scores))
     share = jnp.concatenate(
         [share, jnp.zeros((LANES - heads, requests), jnp.float32)], axis=0
@@ -511,7 +512,6 @@
     row = lax.broadcasted_iota(jnp.int32, (requests, 1), 0).astype(jnp.float32)
     half = LONG_REQS * heads
 
-    outputs.cross()
     values = pool[core].reshape(split, columns)
     old[...] = jnp.dot(near_member, values, preferred_element_type=jnp.float32)
     weighted = jnp.dot(extra[:, :split], values, preferred_element_type=jnp.float32)

time: 47.2 us -> 47.2 us (level)
  no operation moved by 1% of the time
where the time goes in v6:
time: 47.2 us; the launch traced here: 47.1 us
  Pallas kernels  46.4 us (98%)
  between operations  0.7 us (1%)
    pallas_call x1, Pallas kernels, shards(): pl.pallas_call(step_kernel, name='step', out_shape=(jax.ShapeDtypeStruct(...  42.9 us
    pallas_call x1, Pallas kernels, shards(): pl.pallas_call(store_kernel, name='store', out_shape=(jax.ShapeDtypeStruc...  3.55 us

profile of v6, /device:TPU:1, one launch (start us, length us, event | category | flops | bytes accessed | tf_op | source)
XLA Modules:
  0.0 47.1 jit_solution(5775127116575181346)
XLA Ops:
  0.6 0.0 copy-start.1
  0.6 0.0 copy-start.3
  0.7 0.0 copy-start.2
  0.7 0.0 copy-start
  0.7 42.9 %step.1 = (bf16[64,96]{1,0:T(8,128)(2,1)S(1)}, bf16[24,1536]{1,0:T(8,128)(2,1)S(1)}) custom-call(s32[256]{0:T(256)} %context_ref.1, s32[24]{0:T(128)} %owner_ref.1, s32[24]{0:T(128)} %index_ref.1, s32[2,128]{1,0:T(2,128)} %bitcast.4, bf16[96,256]{1,0:T(8,128)(2,1)} %bitcast.6, bf16[1,96]{1,0:T(2,128)(2,1)} %bitcast.7, bf16[3,96,768]{2,1,0:T(8,128)(2,1)} %w_hbm.1, ...), custom_call_target="tpu_custom_call" | custom-call | flops 1000000000 | bytes 4718592 | tf_op jit(solution)/shard_map/step/pallas_call | solution.py:626
  43.5 0.0 copy-done.1
  43.5 0.0 copy-done.3
  43.6 0.0 copy-done.2
  43.6 0.0 copy-done
  43.6 3.6 %store.1 = (bf16[64,96]{1,0:T(8,128)(2,1)}, bf16[24,2,64,768]{3,2,1,0:T(8,128)(2,1)}) custom-call(s32[256]{0:T(256)S(1)} %copy-done.1, s32[24]{0:T(128)S(1)} %copy-done.2, s32[24]{0:T(128)S(1)} %copy-done.3, bf16[64,96]{1,0:T(8,128)(2,1)S(1)} %get-tuple-element.4.hidden_in_ref, bf16[24,1536]{1,0:T(8,128)(2,1)S(1)} %get-tuple-element.5.rows_ref, ...), custom_call_target="tpu_custom_call" | custom-call | tf_op jit(solution)/shard_map/store/pallas_call | solution.py:688
Async XLA Ops:
  0.6 42.9 %copy-start.1 = (s32[256]{0:T(256)S(1)}, s32[256]{0:T(256)}, u32[]{:S(2)}) copy-start(s32[256]{0:T(256)} %context_ref.1) | copy-start | bytes 3076
  0.6 42.9 %copy-start.3 = (s32[24]{0:T(128)S(1)}, s32[24]{0:T(128)}, u32[]{:S(2)}) copy-start(s32[24]{0:T(128)} %index_ref.1) | copy-start | bytes 292
  0.7 42.9 %copy-start.2 = (s32[24]{0:T(128)S(1)}, s32[24]{0:T(128)}, u32[]{:S(2)}) copy-start(s32[24]{0:T(128)} %owner_ref.1) | copy-start | bytes 292
  0.7 42.9 %copy-start = (bf16[24,2,64,768]{3,2,1,0:T(8,128)(2,1)S(1)}, bf16[24,2,64,768]{3,2,1,0:T(8,128)(2,1)}, u32[]{:S(2)}) copy-start(bf16[24,2,64,768]{3,2,1,0:T(8,128)(2,1)} %cache_ref.1) | copy-start | bytes 14155780
